TPU v7x, 32 devices: a whole 2x2x4 slice. The times are simulated.
32 devices in a mesh: tm: 4 (over x, core), lat: 8 (over z, y).
Axes of the slice: x: 2, y: 2, z: 4, core: 2. Of those that a mesh axis runs over, the one named last changes fastest.
Arguments:
- states: float32 [32, 512, 256], P('tm', 'lat'), may hold values from -6 to 6
- multipliers: float32 [32, 512, 256], P('tm', 'lat'), may hold values from -3 to 3
- diffusivity: float32 [512, 256], P('lat'), may hold values from 0.02 to 0.15
- zonal_speed: float32 [512, 256], P('lat'), may hold values from -0.3 to 0.3
- meridional_speed: float32 [512, 256], P('lat'), may hold values from -0.3 to 0.3
- observed_cells: int32 [32, 8, 1024], P('tm', 'lat'), may hold values from 0 to 16383
- observed_values: float32 [32, 8, 1024], P('tm', 'lat'), may hold values from -6 to 6
- observed_weights: float32 [32, 8, 1024], P('tm', 'lat'), may hold values from 0.2 to 2
- fresh_cells: int32 [4, 8, 1024], P(None, 'lat'), may hold values from 0 to 16383
- fresh_values: float32 [4, 8, 1024], P(None, 'lat'), may hold values from -6 to 6
- fresh_weights: float32 [4, 8, 1024], P(None, 'lat'), may hold values from 0.2 to 2
Outputs:
- analysis: float32 [32, 512, 256], P('tm', 'lat')
- lagrange: float32 [32, 512, 256], P('tm', 'lat')
Inputs may be any that keep to these rules, and one draw needn't show every extreme that they name: `observed_cells`: each entry names a cell of its band, counted row by row over the band's 64 x 256 cells; cells may repeat. `fresh_cells`: each entry names a cell of its band, counted row by row over the band's 64 x 256 cells; cells may repeat.
All inputs are finite; a program needn't handle non-finite values.
Results may differ from a plain program's by a relative error of at most 0.000059.
Values sent between devices are 32-bit elements; how exact they have to be, the bound alone decides.
No kernel may reach another device: no remote copies, remote signals or barrier semaphores. Data moves between devices by JAX's collectives and lax.ppermute only.
A program may use at most 64 MiB of HBM per device.

v0:
```python
import functools

import jax
import jax.numpy as jnp
from jax import lax
from jax.experimental import pallas as pl
from jax.experimental.pallas import tpu as pltpu
from jax.sharding import PartitionSpec as P

penalty_weight = 1.0
step_size = 0.15

SUB = 8
MARGIN = 12
LROWS = 9
DROWS = 6
LANES = 128
STEPS = 2
PIECES = 3


def rolled(value, shift, axis):
    return pltpu.roll(value, shift % value.shape[axis], axis)


def sublane(shape):
    return lax.broadcasted_iota(jnp.int32, shape, len(shape) - 2)


def pack_rows(read, base, pairs, offset, write, at):
    for pair in range(pairs):
        first = read(base + 2 * pair)
        second = rolled(read(base + 2 * pair + 1), 4, 0)
        sub = sublane(first.shape)
        write(at + pair, jnp.where((sub >= offset) & (sub < offset + 4), first, second))


def eastward(value):
    half = value.shape[-1] // 2
    axis = value.ndim - 1
    return jnp.concatenate([value[..., half:], rolled(value[..., :half], -1, axis)], axis=axis)


def westward(value):
    half = value.shape[-1] // 2
    axis = value.ndim - 1
    return jnp.concatenate([rolled(value[..., half:], 1, axis), value[..., :half]], axis=axis)


def reordered(value, back=False):
    columns = value.shape[-1]
    natural = lax.broadcasted_iota(jnp.int32, (columns, columns), 1 if back else 0)
    parted = lax.broadcasted_iota(jnp.int32, (columns, columns), 0 if back else 1)
    target = (natural >> 1) + (natural & 1) * (columns // 2)
    moves = jnp.where(target == parted, 1.0, 0.0).astype(jnp.bfloat16)
    total = None
    for piece in reversed(split(value, 3)):
        part = jnp.dot(piece.astype(jnp.bfloat16), moves, preferred_element_type=jnp.float32)
        total = part if total is None else total + part
    return total


def interleave(lines_ref, slot, value):
    rows, columns = value.shape
    for part in range(columns // LANES):
        lines_ref[part, pl.ds(slot, rows, stride=SUB), :] = value[:, part * LANES : (part + 1) * LANES]


def copy_lines(lines_ref, dest_ref):
    rows = dest_ref.shape[0]
    for part in range(lines_ref.shape[0]):
        dest_ref[:, :, part * LANES : (part + 1) * LANES] = lines_ref[part].reshape(rows, SUB, LANES)


def prep_kernel(
    x_ref, l_ref, d_ref, z_ref, m_ref, cells_ref, values_ref, weights_ref,
    xa_ref, la_ref, coef_ref, tn_ref, lines_ref,
):
    slots, rows, columns = x_ref.shape
    for ref, dest in ((x_ref, xa_ref), (l_ref, la_ref)):
        value = reordered(ref[...].reshape(slots * rows, columns))
        for slot in range(slots):
            interleave(lines_ref, slot, value[slot * rows : (slot + 1) * rows])
        copy_lines(lines_ref, dest)
    for kind, ref in enumerate((d_ref, z_ref, m_ref)):
        coef_ref[kind] = reordered(ref[...])
    half = rows // 2

    def pair(step, carry):
        for ref, at in ((xa_ref, 0), (la_ref, half)):
            first = ref[2 * step]
            second = rolled(ref[2 * step + 1], 4, 0)
            tn_ref[at + step] = jnp.where(sublane(first.shape) < 4, first, second)
        return carry

    lax.fori_loop(0, half, pair, 0, unroll=4)
    parts = cells_ref.shape[2] // columns
    for kind, ref in enumerate((cells_ref, values_ref, weights_ref)):
        for slot in range(slots):
            for part in range(parts):
                tn_ref[rows + kind * parts + part, slot : slot + 1, :] = ref[
                    slot, :, part * columns : (part + 1) * columns
                ].astype(jnp.float32)


def split(value, count=PIECES):
    pieces = []
    for _ in range(count):
        piece = value.astype(jnp.bfloat16).astype(jnp.float32)
        pieces.append(piece)
        value = value - piece
    return pieces


def scatter(observed, slots, w_ref, v_ref, w_lines, v_lines):
    rows, _, columns = w_ref.shape
    count = observed(0)[0].shape[1]
    row_ids = lax.broadcasted_iota(jnp.int32, (rows, count), 0)
    column_ids = lax.broadcasted_iota(jnp.int32, (columns, count), 0)
    for slot in range(slots):
        cells, values, weights = observed(slot)
        row_of = cells // columns if columns & (columns - 1) else cells >> (columns.bit_length() - 1)
        column_of = cells - row_of * columns
        column_of = (column_of >> 1) + (column_of & 1) * (columns // 2)
        in_row = row_ids == row_of
        left = jnp.concatenate(
            [
                jnp.where(in_row, piece, 0.0).astype(jnp.bfloat16)
                for piece in split(weights) + split(weights * values)
            ],
            axis=0,
        )
        right = jnp.where(column_ids == column_of, 1.0, 0.0).astype(jnp.bfloat16)
        sums = lax.dot_general(
            left, right, (((1,), (1,)), ((), ())), preferred_element_type=jnp.float32
        )
        for lines, at in ((w_lines, 0), (v_lines, PIECES)):
            total = sums[at * rows : (at + 1) * rows]
            for piece in range(1, PIECES):
                total = total + sums[(at + piece) * rows : (at + piece + 1) * rows]
            interleave(lines, slot, total)
    for slot in range(slots, SUB):
        for lines in (w_lines, v_lines):
            interleave(lines, slot, jnp.zeros((rows, columns), jnp.float32))
    copy_lines(w_lines, w_ref)
    copy_lines(v_lines, v_ref)


def edge_kernel(
    xa_ref, la_ref, coef_ref, cells_ref, values_ref, weights_ref,
    w_ref, v_ref, up_ref, dn_ref, du_ref, dd_ref, d_ref, w_lines, v_lines,
):
    rows, _, columns = xa_ref.shape

    def observed(slot):
        return (cells_ref[slot], values_ref[slot], weights_ref[slot])

    scatter(observed, SUB, w_ref, v_ref, w_lines, v_lines)

    for row in range(DROWS):
        for at, where_row in ((row, rows - DROWS + row), (DROWS + row, row)):
            d_ref[at] = w_ref[where_row] * xa_ref[where_row] - v_ref[where_row]
    for ref, diag, xs, ls, ds in (
        (up_ref, du_ref, rows - MARGIN, rows - LROWS, 0),
        (dn_ref, dd_ref, 0, 0, DROWS),
    ):
        ref[0:MARGIN] = xa_ref[xs : xs + MARGIN]
        ref[MARGIN : MARGIN + LROWS] = la_ref[ls : ls + LROWS]
        ref[MARGIN + LROWS : MARGIN + LROWS + DROWS] = d_ref[ds : ds + DROWS]
        base = MARGIN + LROWS + DROWS
        for kind in range(3):
            flat = coef_ref[kind, xs : xs + MARGIN, :]
            for row in range(MARGIN):
                at = kind * MARGIN + row
                ref[base + at // SUB, at % SUB : at % SUB + 1, :] = flat[row : row + 1]
        for at in range(3 * MARGIN, (ref.shape[0] - base) * SUB):
            ref[base + at // SUB, at % SUB : at % SUB + 1, :] = jnp.zeros((1, columns), jnp.float32)

        def write(at, value, diag=diag):
            diag[at] = value

        lfirst = ls - (LROWS % 2) if ls else 0
        pack_rows(lambda row: xa_ref[row], xs, MARGIN // 2, 0, write, 0)
        pack_rows(lambda row: la_ref[row], lfirst, (LROWS + 1) // 2, 0, write, MARGIN // 2)
        pack_rows(lambda row: d_ref[row], ds, DROWS // 2, 0, write, MARGIN // 2 + (LROWS + 1) // 2)


def next_kernel(
    flag_ref, tn_ref, cells_ref, values_ref, weights_ref, w_ref, v_ref, lists_ref, w_lines, v_lines
):
    last = flag_ref[1] == 1
    rows = w_ref.shape[0]
    pltpu.sync_copy(tn_ref.at[rows : rows + lists_ref.shape[0]], lists_ref)
    parts = lists_ref.shape[0] // 3
    fresh_slots = cells_ref.shape[0]

    def observed(slot):
        out = []
        for kind, ref in enumerate((cells_ref, values_ref, weights_ref)):
            moved = jnp.concatenate(
                [lists_ref[kind * parts + part, slot : slot + 1, :] for part in range(parts)], axis=1
            )
            moved = moved.astype(ref.dtype)
            if slot < fresh_slots:
                moved = jnp.where(last, ref[slot], moved)
            elif kind == 2:
                moved = jnp.where(last, 0.0, moved)
            out.append(moved)
        return out

    scatter(observed, fresh_slots + 1, w_ref, v_ref, w_lines, v_lines)


def sweep_kernel(phase, *refs):
    if phase == 1:
        (flag_ref, xa_ref, la_ref, tn_ref, lo_ref, hi_ref, dlo_ref, dhi_ref, wa_ref, va_ref, wb_ref,
         vb_ref, coef_ref, *refs) = refs
        clo_ref, chi_ref = lo_ref, hi_ref
        (xa2_ref, la2_ref, xb2_ref, lb2_ref, tn2_ref, up_ref, dn_ref, du_ref, dd_ref, *refs) = refs
    else:
        (flag_ref, xa_ref, la_ref, xb_ref, lb_ref, tn_ref, lo_ref, hi_ref, dlo_ref, dhi_ref, wa_ref,
         va_ref, wb_ref, vb_ref, coef_ref, clo_ref, chi_ref, *refs) = refs
        (xout_ref, lout_ref, *refs) = refs
    xs_ref, ls_ref, ws_ref, vs_ref, p_ref, q_ref, flat_ref, cf_ref, lines_ref = refs
    rows, _, columns = xa_ref.shape
    first = flag_ref[0] == 1
    last = flag_ref[1] == 1
    top = MARGIN + rows
    half = rows // 2
    sub = sublane((SUB, columns))

    packed_coef = clo_ref.shape[0] - -(-3 * MARGIN // SUB)
    for kind in range(3):
        flat_ref[kind, MARGIN:top, :] = coef_ref[kind]
        for row in range(MARGIN):
            at = kind * MARGIN + row
            for base, ref in ((0, clo_ref), (top, chi_ref)):
                flat_ref[kind, base + row : base + row + 1, :] = ref[
                    packed_coef + at // SUB, at % SUB : at % SUB + 1, :
                ]
    total = rows + 2 * MARGIN
    diff = flat_ref[0, 0:total, :]
    zonal = 0.5 * flat_ref[1, 0:total, :]
    merid = 0.5 * flat_ref[2, 0:total, :]
    row_global = flag_ref[2] * rows - MARGIN + lax.broadcasted_iota(jnp.int32, diff.shape, 0)
    inside = (row_global >= 0) & (row_global < flag_ref[3] * rows)
    south = diff + merid
    north = diff - merid
    east = diff - zonal
    west = diff + zonal
    planes = (
        1.0 - 4.0 * diff,
        north,
        south,
        east,
        west,
        jnp.where(inside, rolled(south, -1, 0), 0.0),
        jnp.where(inside, rolled(north, 1, 0), 0.0),
        eastward(west),
        westward(east),
    )
    for index, plane in enumerate(planes):
        flat_ref[3 + index, 0:total, :] = plane

    def widen(step, carry):
        start = pl.multiple_of(step * 8, 8)
        for index in range(9):
            block = flat_ref[3 + index, pl.ds(start, 8), :]
            for row in range(8):
                cf_ref[index, start + row] = jnp.broadcast_to(block[row : row + 1], (SUB, columns))
        return carry

    lax.fori_loop(0, total // 8, widen, 0)

    xs_ref[MARGIN:top, 0] = xa_ref[...]
    ls_ref[MARGIN:top, 0] = la_ref[...]
    ws_ref[MARGIN:top, 0] = wa_ref[...]
    vs_ref[MARGIN:top, 0] = va_ref[...]
    ws_ref[MARGIN:top, 1] = wb_ref[...]
    vs_ref[MARGIN:top, 1] = vb_ref[...]
    zero = jnp.zeros((DROWS, 2, SUB, columns), jnp.float32)
    ws_ref[MARGIN - DROWS : MARGIN] = zero
    ws_ref[top : top + DROWS] = zero
    low, high = MARGIN + LROWS, MARGIN + LROWS + DROWS
    for ref, xat, lat_at, dat in (
        (lo_ref, 0, MARGIN - LROWS, MARGIN - DROWS),
        (hi_ref, top, top, top),
    ):
        xs_ref[xat : xat + MARGIN, 0] = ref[0:MARGIN]
        ls_ref[lat_at : lat_at + LROWS, 0] = ref[MARGIN:low]
        vs_ref[dat : dat + DROWS, 0] = -ref[low:high]

    def slot7(value):
        return jnp.broadcast_to(value[SUB - 1 : SUB], value.shape)

    def place(kind, at, pair, source, own, spare):
        dest = {"x": xs_ref, "l": ls_ref, "d": vs_ref}[kind]
        for odd, value in ((0, source), (1, rolled(source, 4, 0))):
            row = at + 2 * pair + odd
            if phase == 2:
                if kind == "d":
                    other = spare if odd == 0 else rolled(spare, 4, 0)
                    value = jnp.where(last, other, value)
                value = jnp.where(sub < 2, own(2 * pair + odd), value)
                if kind == "x":
                    value = jnp.where(last, slot7(xs_ref[row, 0]), value)
                elif kind == "l":
                    value = jnp.where(last, 0.0, value)
            dest[row, 1] = -value if kind == "d" else value

    own_x = (lambda row: xb_ref[row]) if phase == 2 else None
    own_l = (lambda row: lb_ref[row]) if phase == 2 else None

    def interior(step, carry):
        place("x", MARGIN, step, tn_ref[step], own_x, None)
        place("l", MARGIN, step, tn_ref[half + step], own_l, None)
        return carry

    lax.fori_loop(0, half, interior, 0, unroll=2)
    lpairs = (LROWS + 1) // 2
    dbase = MARGIN // 2 + lpairs
    for ref, diag, at, lat_at, lskip, dat in (
        (lo_ref, dlo_ref, 0, MARGIN - 2 * lpairs, 1, MARGIN - DROWS),
        (hi_ref, dhi_ref, top, top, 0, top),
    ):
        for pair in range(MARGIN // 2):
            place("x", at, pair, diag[pair], lambda row, ref=ref: ref[row], None)
        for pair in range(lpairs):
            place(
                "l", lat_at, pair, diag[MARGIN // 2 + pair],
                lambda row, ref=ref, lskip=lskip: ref[
                    MARGIN + min(max(row - lskip, 0), LROWS - 1)
                ],
                None,
            )
        for pair in range(DROWS // 2):
            spare = ref[high + pair] if phase == 2 else None
            place(
                "d", dat, pair, diag[dbase + pair], lambda row, ref=ref: ref[low + row], spare
            )

    keep = jnp.logical_not(last)
    if phase == 2:
        keep = keep | (sub < 4)
    else:
        keep = keep & (sub < SUB)
    frozen = first & (sub < 4)

    def stencil(src, adjoint, reach, finish):
        base = 5 if adjoint else 1
        start = MARGIN - reach
        block = pl.cdiv(rows + 2 * reach, STEPS)

        def step(index, carry):
            row0 = start + index * block
            for row in range(block):
                at = row0 + row
                coef = [cf_ref[k, at] for k in (0, base, base + 1, base + 2, base + 3)]
                out = []
                for tile in range(2):
                    value = src[at, tile]
                    out.append(
                        coef[0] * value
                        + coef[1] * src[at + 1, tile]
                        + coef[2] * src[at - 1, tile]
                        + coef[3] * eastward(value)
                        + coef[4] * westward(value)
                    )
                finish(at, out)
            return carry

        lax.fori_loop(0, STEPS, step, 0)

    def store(dest):
        def finish(at, out):
            dest[at, 0] = out[0]
            dest[at, 1] = out[1]

        return finish

    def forward_end(at, out):
        ahead_a = rolled(out[0], 1, 0)
        ahead_b = rolled(out[1], 1, 0)
        ahead_b = jnp.where(sub == 0, ahead_a, ahead_b)
        jump_a = jnp.where(sub == 0, 0.0, xs_ref[at, 0] - ahead_a)
        jump_b = xs_ref[at, 1] - ahead_b
        ls_ref[at, 0] = ls_ref[at, 0] + jump_a
        ls_ref[at, 1] = jnp.where(keep, ls_ref[at, 1] + jump_b, 0.0)

    def backward_end(at, out):
        back_a = rolled(out[0], -1, 0)
        back_b = rolled(out[1], -1, 0)
        back_a = jnp.where(sub == SUB - 1, back_b, back_a)
        for tile, after in ((0, back_a), (1, back_b)):
            value = xs_ref[at, tile]
            gradient = ws_ref[at, tile] * value - vs_ref[at, tile] + ls_ref[at, tile] - after
            new = value - step_size * gradient
            if phase == 2 and tile == 0:
                new = jnp.where(frozen, value, new)
            xs_ref[at, tile] = new

    for reach in (MARGIN, MARGIN // 2):
        stencil(xs_ref, False, reach - 1, store(p_ref))
        stencil(p_ref, False, reach - 2, store(q_ref))
        stencil(q_ref, False, reach - 3, forward_end)
        stencil(ls_ref, True, reach - 4, store(p_ref))
        stencil(p_ref, True, reach - 5, store(q_ref))
        stencil(q_ref, True, reach - 6, backward_end)

    if phase == 2:
        parts = columns // LANES
        for ref, dest in ((xs_ref, xout_ref), (ls_ref, lout_ref)):

            def gather(step, carry, ref=ref):
                value = jnp.where(
                    sub < 4,
                    rolled(ref[MARGIN + step, 0], 4, 0),
                    rolled(ref[MARGIN + step, 1], 4, 0),
                )
                for part in range(parts):
                    lines_ref[part, pl.ds(pl.multiple_of(step * SUB, SUB), SUB), :] = value[
                        :, part * LANES : (part + 1) * LANES
                    ]
                return carry

            lax.fori_loop(0, rows, gather, 0, unroll=4)
            value = jnp.concatenate(
                [
                    jnp.concatenate(
                        [lines_ref[part, pl.ds(slot, rows, stride=SUB), :] for part in range(parts)],
                        axis=1,
                    )
                    for slot in range(SUB)
                ],
                axis=0,
            )
            dest[...] = reordered(value, back=True).reshape(dest.shape)
        return

    def fix(step, carry):
        at = MARGIN + step
        value = xs_ref[at, 1]
        xs_ref[at, 1] = jnp.where(last, slot7(xs_ref[at, 0]), value)
        return carry

    lax.fori_loop(0, rows, fix, 0, unroll=4)
    xa2_ref[...] = xs_ref[MARGIN:top, 0]
    la2_ref[...] = ls_ref[MARGIN:top, 0]
    xb2_ref[...] = xs_ref[MARGIN:top, 1]
    lb2_ref[...] = ls_ref[MARGIN:top, 1]

    def packed(ref, at, tile):
        second = rolled(ref[at + 1, tile], 4, 0)
        return jnp.where((sub >= 2) & (sub < 6), ref[at, tile], second)

    def send(step, carry):
        tn2_ref[step] = packed(xs_ref, MARGIN + 2 * step, 0)
        tn2_ref[half + step] = packed(ls_ref, MARGIN + 2 * step, 0)
        return carry

    lax.fori_loop(0, half, send, 0, unroll=2)

    def owned(ref, at):
        return jnp.where(sub < 2, ref[at, 1], ref[at, 0])

    for ref, diag, xat, lat_at, lfirst, dat in (
        (up_ref, du_ref, top - MARGIN, top - LROWS, top - 2 * lpairs, top - DROWS),
        (dn_ref, dd_ref, MARGIN, MARGIN, MARGIN, MARGIN),
    ):
        for row in range(DROWS):
            at = dat + row
            for tile in range(2):
                p_ref[at, tile] = ws_ref[at, tile] * xs_ref[at, tile] - vs_ref[at, tile]
        for row in range(MARGIN):
            ref[row] = owned(xs_ref, xat + row)
        for row in range(LROWS):
            ref[MARGIN + row] = owned(ls_ref, lat_at + row)
        for row in range(DROWS):
            ref[low + row] = owned(p_ref, dat + row)
        for pair in range(DROWS // 2):
            ref[high + pair] = packed(p_ref, dat + 2 * pair, 1)
        for pair in range(MARGIN // 2):
            diag[pair] = packed(xs_ref, xat + 2 * pair, 0)
        for pair in range(lpairs):
            diag[MARGIN // 2 + pair] = packed(ls_ref, lfirst + 2 * pair, 0)
        for pair in range(DROWS // 2):
            diag[dbase + pair] = packed(p_ref, dat + 2 * pair, 0)


def body(
    states,
    multipliers,
    diffusivity,
    zonal_speed,
    meridional_speed,
    observed_cells,
    observed_values,
    observed_weights,
    fresh_cells,
    fresh_values,
    fresh_weights,
):
    slots, rows, columns = states.shape
    half = fresh_cells.shape[0]
    tm_count, lat_count = lax.axis_size("tm"), lax.axis_size("lat")
    tm_index, lat_index = lax.axis_index("tm"), lax.axis_index("lat")
    flags = jnp.stack(
        [
            (tm_index == 0).astype(jnp.int32),
            (tm_index == tm_count - 1).astype(jnp.int32),
            lat_index.astype(jnp.int32),
            jnp.int32(lat_count),
        ]
    )

    def send(value, tm_step, lat_step):
        pairs = []
        for t in range(tm_count):
            for b in range(lat_count):
                to_t, to_b = t + tm_step, b + lat_step
                if 0 <= to_t < tm_count and 0 <= to_b < lat_count:
                    pairs.append((t * lat_count + b, to_t * lat_count + to_b))
        return lax.ppermute(value, ("tm", "lat"), pairs)

    smem = pl.BlockSpec(memory_space=pltpu.SMEM)
    vmem = pl.BlockSpec(memory_space=pltpu.VMEM)

    def call(kernel, outs, args, scratch=(), flagged=False, hbm=()):
        specs = [vmem] * len(args)
        for index in hbm:
            specs[index] = pl.BlockSpec(memory_space=pl.ANY)
        if flagged:
            args, specs = (flags, *args), [smem] + specs
        return pl.pallas_call(
            kernel,
            out_shape=[jax.ShapeDtypeStruct(shape, jnp.float32) for shape in outs],
            in_specs=specs,
            out_specs=[vmem] * len(outs),
            scratch_shapes=list(scratch),
        )(*args)

    tile = (SUB, columns)
    lines = pltpu.VMEM((columns // LANES, rows * SUB, LANES), jnp.float32)
    field = (rows, *tile)
    count = observed_cells.shape[-1]
    lists = 3 * (count // columns)
    diag = (MARGIN // 2 + (LROWS + 1) // 2 + DROWS // 2, *tile)
    edge = MARGIN + LROWS + DROWS
    coef_rows = -(-3 * MARGIN // SUB)

    obs = (observed_cells, observed_values, observed_weights)

    xa, la, coef, tn = call(
        prep_kernel,
        (field, field, (3, rows, columns), (rows + lists, *tile)),
        (states, multipliers, diffusivity, zonal_speed, meridional_speed, *obs),
        (lines,),
    )
    tn = send(tn, -1, 0)
    wa, va, up, dn, du, dd = call(
        edge_kernel,
        (field, field, (edge + coef_rows, *tile), (edge + coef_rows, *tile), diag, diag),
        (xa, la, coef, *obs),
        (pltpu.VMEM((2 * DROWS, *tile), jnp.float32), lines, lines),
    )
    lo = send(up, 0, 1)
    hi = send(dn, 0, -1)
    dlo = send(du, -1, 1)
    dhi = send(dd, -1, -1)

    wb, vb = call(
        next_kernel,
        (field, field),
        (tn, fresh_cells, fresh_values, fresh_weights),
        (pltpu.VMEM((lists, *tile), jnp.float32), lines, lines),
        flagged=True,
        hbm=(0,),
    )
    obs = (wa, va, wb, vb)
    coef_halos = (lo, hi)

    reach = rows + 2 * MARGIN + 8
    scratch = (
        [pltpu.VMEM((reach, 2, *tile), jnp.float32)] * 6
        + [pltpu.VMEM((12, reach, columns), jnp.float32)]
        + [pltpu.VMEM((9, reach, *tile), jnp.float32), lines]
    )
    edge2 = (edge + DROWS // 2, *tile)
    xa2, la2, xb2, lb2, tn2, up, dn, du, dd = call(
        functools.partial(sweep_kernel, 1),
        (field, field, field, field, field, edge2, edge2, diag, diag),
        (xa, la, tn, lo, hi, dlo, dhi, *obs, coef),
        scratch,
        flagged=True,
    )
    tn2 = send(tn2, -1, 0)
    lo = send(up, 0, 1)
    hi = send(dn, 0, -1)
    dlo = send(du, -1, 1)
    dhi = send(dd, -1, -1)
    analysis, lagrange = call(
        functools.partial(sweep_kernel, 2),
        (states.shape, states.shape),
        (xa2, la2, xb2, lb2, tn2, lo, hi, dlo, dhi, *obs, coef, *coef_halos),
        scratch,
        flagged=True,
    )
    return (analysis, lagrange)


def solution(mesh):
    in_specs = (
        P("tm", "lat", None),
        P("tm", "lat", None),
        P("lat", None),
        P("lat", None),
        P("lat", None),
        P("tm", "lat", None),
        P("tm", "lat", None),
        P("tm", "lat", None),
        P(None, "lat", None),
        P(None, "lat", None),
        P(None, "lat", None),
    )
    out_specs = (P("tm", "lat", None), P("tm", "lat", None))
    return jax.shard_map(body, mesh=mesh, in_specs=in_specs, out_specs=out_specs, check_vma=False)
```

profile of v0, /device:TPU:16, one launch (start us, length us, event | category | flops | bytes accessed | tf_op | source)
XLA Modules:
  0.0 83.2 jit_solution(6724015065622302338)
XLA Ops:
  0.6 3.4 %shard_map.122 = (f32[64,8,256]{2,1,0:T(8,128)}, f32[64,8,256]{2,1,0:T(8,128)}, f32[3,64,256]{2,1,0:T(8,128)}, f32[76,8,256]{2,1,0:T(8,128)}) custom-call(f32[8,64,256]{2,1,0:T(8,128)} %x_ref.1, f32[8,64,256]{2,1,0:T(8,128)} %l_ref.1, f32[64,256]{1,0:T(8,128)} %d_ref.1, f32[64,256]{1,0:T(8,128)} %z_ref.1, f32[64,256]{1,0:T(8,128)} %m_ref.1, ...), custom_call_target="tpu_custom_call" | custom-call | tf_op jit(solution)/shard_map/pallas_call | solution.py:534
  4.1 1.3 %collective-permute-start = (f32[76,8,256]{2,1,0:T(8,128)}, f32[76,8,256]{2,1,0:T(8,128)S(1)}, u32[]{:S(2)}, u32[]{:S(2)}) collective-permute-start(f32[76,8,256]{2,1,0:T(8,128)} %get-tuple-element.25), channel_id=1, source_target_pairs={{8,0},{9,1},{10,2},{11,3},{12,4},{13,5},{14,6},{15,7},{16,8},{17,9... | collective-permute-start | bytes 1867784 | tf_op jit(solution)/shard_map/ppermute | solution.py:523
  5.4 4.4 %shard_map.123 = (f32[64,8,256]{2,1,0:T(8,128)}, f32[64,8,256]{2,1,0:T(8,128)}, f32[32,8,256]{2,1,0:T(8,128)}, f32[32,8,256]{2,1,0:T(8,128)}, f32[14,8,256]{2,1,0:T(8,128)}, /*index=5*/f32[14,8,256]{2,1,0:T(8,128)}) custom-call(f32[64,8,256]{2,1,0:T(8,128)} %get-tuple-element.23.xa_ref.refs_1_, f32[64,8,256]{2,1,0:T(8,128)} %get-tuple-element.24.la_ref.refs_2_, ...), custom_call_target="tpu_custom_call" | custom-call | tf_op jit(solution)/shard_map/pallas_call | solution.py:534
  9.7 3.4 %collective-permute-start.1 = (f32[32,8,256]{2,1,0:T(8,128)}, f32[32,8,256]{2,1,0:T(8,128)S(1)}, u32[]{:S(2)}, u32[]{:S(2)}) collective-permute-start(f32[32,8,256]{2,1,0:T(8,128)} %get-tuple-element.27), channel_id=1, source_target_pairs={{0,1},{1,2},{2,3},{3,4},{4,5},{5,6},{6,7},{8,9},{9,10},{10,11},{11... | collective-permute-start | bytes 786440 | tf_op jit(solution)/shard_map/ppermute | solution.py:523
  13.2 3.3 %collective-permute-start.2 = (f32[32,8,256]{2,1,0:T(8,128)}, f32[32,8,256]{2,1,0:T(8,128)S(1)}, u32[]{:S(2)}, u32[]{:S(2)}) collective-permute-start(f32[32,8,256]{2,1,0:T(8,128)} %get-tuple-element.28), channel_id=1, source_target_pairs={{1,0},{2,1},{3,2},{4,3},{5,4},{6,5},{7,6},{9,8},{10,9},{11,10},{12... | collective-permute-start | bytes 786440 | tf_op jit(solution)/shard_map/ppermute | solution.py:523
  16.5 1.3 %collective-permute-start.3 = (f32[14,8,256]{2,1,0:T(8,128)}, f32[14,8,256]{2,1,0:T(8,128)S(1)}, u32[]{:S(2)}, u32[]{:S(2)}) collective-permute-start(f32[14,8,256]{2,1,0:T(8,128)} %get-tuple-element.29), channel_id=1, source_target_pairs={{8,1},{9,2},{10,3},{11,4},{12,5},{13,6},{14,7},{16,9},{17,10},{18,... | collective-permute-start | bytes 344072 | tf_op jit(solution)/shard_map/ppermute | solution.py:523
  17.8 1.3 %collective-permute-start.4 = (f32[14,8,256]{2,1,0:T(8,128)}, f32[14,8,256]{2,1,0:T(8,128)S(1)}, u32[]{:S(2)}, u32[]{:S(2)}) collective-permute-start(f32[14,8,256]{2,1,0:T(8,128)} %get-tuple-element.30), channel_id=1, source_target_pairs={{9,0},{10,1},{11,2},{12,3},{13,4},{14,5},{15,6},{17,8},{18,9},{19,... | collective-permute-start | bytes 344072 | tf_op jit(solution)/shard_map/ppermute | solution.py:523
  19.1 0.7 pad_add_fusion.flag_ref.refs_0_
  19.8 0.0 collective-permute-done.tn_ref.refs_3_
  19.8 0.8 %copy-done = f32[76,8,256]{2,1,0:T(8,128)} copy-done((f32[76,8,256]{2,1,0:T(8,128)}, f32[76,8,256]{2,1,0:T(8,128)S(1)}, u32[]{:S(2)}) %copy-start) | copy-done | bytes 622616
  20.6 4.0 %shard_map.124 = (f32[64,8,256]{2,1,0:T(8,128)}, f32[64,8,256]{2,1,0:T(8,128)}) custom-call(s32[4]{0:T(128)} %pad_add_fusion.flag_ref.refs_0_, f32[76,8,256]{2,1,0:T(8,128)} %copy-done, s32[4,1,1024]{2,1,0:T(1,128)} %cells_ref.5, f32[4,1,1024]{2,1,0:T(1,128)} %values_ref.5, f32[4,1,1024]{2,1,0:T(1,128)} %weights_ref.5), custom_call_target="tpu_custom_call" | custom-call | tf_op jit(solution)/shard_map/pallas_call | solution.py:534
  24.6 7.8 %collective-permute-done.4.refs_7_ = f32[14,8,256]{2,1,0:T(8,128)S(1)} collective-permute-done((f32[14,8,256]{2,1,0:T(8,128)}, f32[14,8,256]{2,1,0:T(8,128)S(1)}, u32[]{:S(2)}, u32[]{:S(2)}) %collective-permute-start.4) | collective-permute-done | bytes 114720 | tf_op jit(solution)/shard_map/ppermute | solution.py:523
  32.5 0.0 collective-permute-done.1.refs_4_.refs_15_
  32.5 0.0 collective-permute-done.2.refs_5_.refs_16_
  32.5 0.6 copy-done.7
  33.1 0.1 copy-done.1
  33.2 0.1 copy-done.2
  33.3 12.5 %shard_map.125 = (f32[64,8,256]{2,1,0:T(8,128)}, f32[64,8,256]{2,1,0:T(8,128)}, f32[64,8,256]{2,1,0:T(8,128)}, f32[64,8,256]{2,1,0:T(8,128)}, f32[64,8,256]{2,1,...) custom-call(s32[4]{0:T(128)} %pad_add_fusion.flag_ref.refs_0_, ...), custom_call_target="tpu_custom_call" | custom-call | tf_op jit(solution)/shard_map/pallas_call | solution.py:534
  45.8 1.3 %collective-permute-start.5 = (f32[64,8,256]{2,1,0:T(8,128)}, f32[64,8,256]{2,1,0:T(8,128)S(1)}, u32[]{:S(2)}, u32[]{:S(2)}) collective-permute-start(f32[64,8,256]{2,1,0:T(8,128)} %get-tuple-element.39), channel_id=1, source_target_pairs={{8,0},{9,1},{10,2},{11,3},{12,4},{13,5},{14,6},{15,7},{16,8},{17,9... | collective-permute-start | bytes 1572872 | tf_op jit(solution)/shard_map/ppermute | solution.py:523
  47.1 2.6 %collective-permute-start.6 = (f32[30,8,256]{2,1,0:T(8,128)}, f32[30,8,256]{2,1,0:T(8,128)S(1)}, u32[]{:S(2)}, u32[]{:S(2)}) collective-permute-start(f32[30,8,256]{2,1,0:T(8,128)} %get-tuple-element.40), channel_id=1, source_target_pairs={{0,1},{1,2},{2,3},{3,4},{4,5},{5,6},{6,7},{8,9},{9,10},{10,11},{11... | collective-permute-start | bytes 737288 | tf_op jit(solution)/shard_map/ppermute | solution.py:523
  49.7 4.2 %collective-permute-start.7 = (f32[30,8,256]{2,1,0:T(8,128)}, f32[30,8,256]{2,1,0:T(8,128)S(1)}, u32[]{:S(2)}, u32[]{:S(2)}) collective-permute-start(f32[30,8,256]{2,1,0:T(8,128)} %get-tuple-element.41), channel_id=1, source_target_pairs={{1,0},{2,1},{3,2},{4,3},{5,4},{6,5},{7,6},{9,8},{10,9},{11,10},{12... | collective-permute-start | bytes 737288 | tf_op jit(solution)/shard_map/ppermute | solution.py:523
  53.8 1.3 %collective-permute-start.8 = (f32[14,8,256]{2,1,0:T(8,128)}, f32[14,8,256]{2,1,0:T(8,128)S(1)}, u32[]{:S(2)}, u32[]{:S(2)}) collective-permute-start(f32[14,8,256]{2,1,0:T(8,128)} %get-tuple-element.42), channel_id=1, source_target_pairs={{8,1},{9,2},{10,3},{11,4},{12,5},{13,6},{14,7},{16,9},{17,10},{18,... | collective-permute-start | bytes 344072 | tf_op jit(solution)/shard_map/ppermute | solution.py:523
  55.1 1.5 %collective-permute-start.9 = (f32[14,8,256]{2,1,0:T(8,128)}, f32[14,8,256]{2,1,0:T(8,128)S(1)}, u32[]{:S(2)}, u32[]{:S(2)}) collective-permute-start(f32[14,8,256]{2,1,0:T(8,128)} %get-tuple-element.43), channel_id=1, source_target_pairs={{9,0},{10,1},{11,2},{12,3},{13,4},{14,5},{15,6},{17,8},{18,9},{19,... | collective-permute-start | bytes 344072 | tf_op jit(solution)/shard_map/ppermute | solution.py:523
  56.6 4.5 %collective-permute-done.8.refs_8_ = f32[14,8,256]{2,1,0:T(8,128)S(1)} collective-permute-done((f32[14,8,256]{2,1,0:T(8,128)}, f32[14,8,256]{2,1,0:T(8,128)S(1)}, u32[]{:S(2)}, u32[]{:S(2)}) %collective-permute-start.8) | collective-permute-done | bytes 114720 | tf_op jit(solution)/shard_map/ppermute | solution.py:523
  61.2 7.9 %collective-permute-done.9.refs_9_ = f32[14,8,256]{2,1,0:T(8,128)S(1)} collective-permute-done((f32[14,8,256]{2,1,0:T(8,128)}, f32[14,8,256]{2,1,0:T(8,128)S(1)}, u32[]{:S(2)}, u32[]{:S(2)}) %collective-permute-start.9) | collective-permute-done | bytes 114720 | tf_op jit(solution)/shard_map/ppermute | solution.py:523
  69.1 0.0 collective-permute-done.6.refs_6_
  69.1 0.0 collective-permute-done.5.refs_5_
  69.2 0.6 copy-done.9
  69.7 0.1 copy-done.4
  69.8 0.1 copy-done.5
  69.9 0.2 copy-done.3
  70.1 13.1 %shard_map.126 = (f32[8,64,256]{2,1,0:T(8,128)}, f32[8,64,256]{2,1,0:T(8,128)}) custom-call(s32[4]{0:T(128)} %pad_add_fusion.flag_ref.refs_0_, f32[64,8,256]{2,1,0:T(8,128)} %get-tuple-element.35.refs_1_, f32[64,8,256]{2,1,0:T(8,128)} %get-tuple-element.36.refs_2_, f32[64,8,256]{2,1,0:T(8,128)} %get-tuple-element.37.refs_3_, ...), custom_call_target="tpu_custom_call" | custom-call | tf_op jit(solution)/shard_map/pallas_call | solution.py:534
  (14 shorter events, 0.0 us)
Async XLA Ops:
  4.1 15.7 %collective-permute-start = (f32[76,8,256]{2,1,0:T(8,128)}, f32[76,8,256]{2,1,0:T(8,128)S(1)}, u32[]{:S(2)}, u32[]{:S(2)}) collective-permute-start(f32[76,8,256]{2,1,0:T(8,128)} %get-tuple-element.25), channel_id=1, source_target_pairs={{8,0},{9,1},{10,2},{11,3},{12,4},{13,5},{14,6},{15,7},{16,8},{17,9... | collective-permute-start | bytes 1867784 | tf_op jit(solution)/shard_map/ppermute | solution.py:523
  9.7 22.7 %collective-permute-start.1 = (f32[32,8,256]{2,1,0:T(8,128)}, f32[32,8,256]{2,1,0:T(8,128)S(1)}, u32[]{:S(2)}, u32[]{:S(2)}) collective-permute-start(f32[32,8,256]{2,1,0:T(8,128)} %get-tuple-element.27), channel_id=1, source_target_pairs={{0,1},{1,2},{2,3},{3,4},{4,5},{5,6},{6,7},{8,9},{9,10},{10,11},{11... | collective-permute-start | bytes 786440 | tf_op jit(solution)/shard_map/ppermute | solution.py:523
  13.2 19.3 %collective-permute-start.2 = (f32[32,8,256]{2,1,0:T(8,128)}, f32[32,8,256]{2,1,0:T(8,128)S(1)}, u32[]{:S(2)}, u32[]{:S(2)}) collective-permute-start(f32[32,8,256]{2,1,0:T(8,128)} %get-tuple-element.28), channel_id=1, source_target_pairs={{1,0},{2,1},{3,2},{4,3},{5,4},{6,5},{7,6},{9,8},{10,9},{11,10},{12... | collective-permute-start | bytes 786440 | tf_op jit(solution)/shard_map/ppermute | solution.py:523
  16.5 8.1 %collective-permute-start.3 = (f32[14,8,256]{2,1,0:T(8,128)}, f32[14,8,256]{2,1,0:T(8,128)S(1)}, u32[]{:S(2)}, u32[]{:S(2)}) collective-permute-start(f32[14,8,256]{2,1,0:T(8,128)} %get-tuple-element.29), channel_id=1, source_target_pairs={{8,1},{9,2},{10,3},{11,4},{12,5},{13,6},{14,7},{16,9},{17,10},{18,... | collective-permute-start | bytes 344072 | tf_op jit(solution)/shard_map/ppermute | solution.py:523
  17.8 14.7 %collective-permute-start.4 = (f32[14,8,256]{2,1,0:T(8,128)}, f32[14,8,256]{2,1,0:T(8,128)S(1)}, u32[]{:S(2)}, u32[]{:S(2)}) collective-permute-start(f32[14,8,256]{2,1,0:T(8,128)} %get-tuple-element.30), channel_id=1, source_target_pairs={{9,0},{10,1},{11,2},{12,3},{13,4},{14,5},{15,6},{17,8},{18,9},{19,... | collective-permute-start | bytes 344072 | tf_op jit(solution)/shard_map/ppermute | solution.py:523
  19.8 0.9 %copy-start = (f32[76,8,256]{2,1,0:T(8,128)}, f32[76,8,256]{2,1,0:T(8,128)S(1)}, u32[]{:S(2)}) copy-start(f32[76,8,256]{2,1,0:T(8,128)S(1)} %collective-permute-done.tn_ref.refs_3_) | copy-start | bytes 1867780
  24.6 7.9 %copy-start.6 = (f32[14,8,256]{2,1,0:T(8,128)}, f32[14,8,256]{2,1,0:T(8,128)S(1)}, u32[]{:S(2)}) copy-start(f32[14,8,256]{2,1,0:T(8,128)S(1)} %collective-permute-done.3.refs_6_) | copy-start | bytes 344068
  32.5 0.6 copy-start.7
  32.5 0.7 copy-start.1
  32.5 0.8 copy-start.2
  45.8 23.3 %collective-permute-start.5 = (f32[64,8,256]{2,1,0:T(8,128)}, f32[64,8,256]{2,1,0:T(8,128)S(1)}, u32[]{:S(2)}, u32[]{:S(2)}) collective-permute-start(f32[64,8,256]{2,1,0:T(8,128)} %get-tuple-element.39), channel_id=1, source_target_pairs={{8,0},{9,1},{10,2},{11,3},{12,4},{13,5},{14,6},{15,7},{16,8},{17,9... | collective-permute-start | bytes 1572872 | tf_op jit(solution)/shard_map/ppermute | solution.py:523
  47.1 22.0 %collective-permute-start.6 = (f32[30,8,256]{2,1,0:T(8,128)}, f32[30,8,256]{2,1,0:T(8,128)S(1)}, u32[]{:S(2)}, u32[]{:S(2)}) collective-permute-start(f32[30,8,256]{2,1,0:T(8,128)} %get-tuple-element.40), channel_id=1, source_target_pairs={{0,1},{1,2},{2,3},{3,4},{4,5},{5,6},{6,7},{8,9},{9,10},{10,11},{11... | collective-permute-start | bytes 737288 | tf_op jit(solution)/shard_map/ppermute | solution.py:523
  49.7 19.5 %collective-permute-start.7 = (f32[30,8,256]{2,1,0:T(8,128)}, f32[30,8,256]{2,1,0:T(8,128)S(1)}, u32[]{:S(2)}, u32[]{:S(2)}) collective-permute-start(f32[30,8,256]{2,1,0:T(8,128)} %get-tuple-element.41), channel_id=1, source_target_pairs={{1,0},{2,1},{3,2},{4,3},{5,4},{6,5},{7,6},{9,8},{10,9},{11,10},{12... | collective-permute-start | bytes 737288 | tf_op jit(solution)/shard_map/ppermute | solution.py:523
  53.8 7.3 %collective-permute-start.8 = (f32[14,8,256]{2,1,0:T(8,128)}, f32[14,8,256]{2,1,0:T(8,128)S(1)}, u32[]{:S(2)}, u32[]{:S(2)}) collective-permute-start(f32[14,8,256]{2,1,0:T(8,128)} %get-tuple-element.42), channel_id=1, source_target_pairs={{8,1},{9,2},{10,3},{11,4},{12,5},{13,6},{14,7},{16,9},{17,10},{18,... | collective-permute-start | bytes 344072 | tf_op jit(solution)/shard_map/ppermute | solution.py:523
  55.1 14.0 %collective-permute-start.9 = (f32[14,8,256]{2,1,0:T(8,128)}, f32[14,8,256]{2,1,0:T(8,128)S(1)}, u32[]{:S(2)}, u32[]{:S(2)}) collective-permute-start(f32[14,8,256]{2,1,0:T(8,128)} %get-tuple-element.43), channel_id=1, source_target_pairs={{9,0},{10,1},{11,2},{12,3},{13,4},{14,5},{15,6},{17,8},{18,9},{19,... | collective-permute-start | bytes 344072 | tf_op jit(solution)/shard_map/ppermute | solution.py:523
  61.2 8.0 %copy-start.8 = (f32[14,8,256]{2,1,0:T(8,128)}, f32[14,8,256]{2,1,0:T(8,128)S(1)}, u32[]{:S(2)}) copy-start(f32[14,8,256]{2,1,0:T(8,128)S(1)} %collective-permute-done.8.refs_8_) | copy-start | bytes 344068
  69.1 0.6 copy-start.9
  69.1 0.7 copy-start.4
  69.1 0.8 copy-start.5
  69.1 1.0 %copy-start.3 = (f32[64,8,256]{2,1,0:T(8,128)}, f32[64,8,256]{2,1,0:T(8,128)S(1)}, u32[]{:S(2)}) copy-start(f32[64,8,256]{2,1,0:T(8,128)S(1)} %collective-permute-done.5.refs_5_) | copy-start | bytes 1572868
where the time goes:
time: 83.7 us; the launch traced here: 83.2 us
  Pallas kernels  37.4 us (45%)
  starting transfers between devices  21.4 us (26%)
  waiting for transfers between devices  20.3 us (24%)
  local copies, waits for them, and re-layouts  2.63 us (3%)
    pallas_call x5, Pallas kernels, call(): pl.pallas_call(kernel, out_shape=[jax.ShapeDtypeStruct(shape, jnp.float32...  37.4 us
    ppermute x10, starting transfers between devices, send(): return lax.ppermute(value, ('tm', 'lat'), pairs)  21.4 us
    ppermute x10, waiting for transfers between devices, send(): return lax.ppermute(value, ('tm', 'lat'), pairs)  20.3 us
    unnamed x20, local copies, waits for them, and re-layouts  2.63 us
  transfers between devices with their start and end apart: 10, of which 3 were waited for; matrix products, arithmetic and copies ran while one was open for 1% of the time, Pallas kernels for 10%

commit v1 on v0

v1 whole, which is shorter than its diff:
```python
import jax
import jax.numpy as jnp
from jax import lax
from jax.experimental import pallas as pl
from jax.experimental.pallas import tpu as pltpu
from jax.sharding import PartitionSpec as P

penalty_weight = 1.0
step_size = 0.15

SUB = 8
MARGIN = 12
LROWS = 9
DROWS = 6
EDGE = MARGIN + LROWS + DROWS
PAIRS = MARGIN // 2 + (LROWS + 1) // 2 + DROWS // 2
STRIP = 3 * MARGIN
LANES = 128
PIECES = 3


def rolled(value, shift, axis):
    return pltpu.roll(value, shift % value.shape[axis], axis)


def sublane(shape):
    return lax.broadcasted_iota(jnp.int32, shape, len(shape) - 2)


def two_rows(first, second):
    sub = sublane(first.shape)
    return jnp.where((sub >= 2) & (sub < 6), first, rolled(second, 4, 0))


def eastward(value):
    half = value.shape[-1] // 2
    axis = value.ndim - 1
    return jnp.concatenate([value[..., half:], rolled(value[..., :half], -1, axis)], axis=axis)


def westward(value):
    half = value.shape[-1] // 2
    axis = value.ndim - 1
    return jnp.concatenate([rolled(value[..., half:], 1, axis), value[..., :half]], axis=axis)


def reordered(value, back=False):
    columns = value.shape[-1]
    natural = lax.broadcasted_iota(jnp.int32, (columns, columns), 1 if back else 0)
    parted = lax.broadcasted_iota(jnp.int32, (columns, columns), 0 if back else 1)
    target = (natural >> 1) + (natural & 1) * (columns // 2)
    moves = jnp.where(target == parted, 1.0, 0.0).astype(jnp.bfloat16)
    total = None
    for piece in reversed(split(value, 3)):
        part = jnp.dot(piece.astype(jnp.bfloat16), moves, preferred_element_type=jnp.float32)
        total = part if total is None else total + part
    return total


def interleave(lines_ref, slot, value):
    rows, columns = value.shape
    for part in range(columns // LANES):
        lines_ref[part, pl.ds(slot, rows, stride=SUB), :] = value[:, part * LANES : (part + 1) * LANES]


def copy_lines(lines_ref, dest_ref):
    rows = dest_ref.shape[0]
    for part in range(lines_ref.shape[0]):
        dest_ref[:, :, part * LANES : (part + 1) * LANES] = lines_ref[part].reshape(rows, SUB, LANES)


def prep_kernel(
    x_ref, l_ref, d_ref, z_ref, m_ref, cells_ref, values_ref, weights_ref,
    tn_ref, coef_ref, lines_ref,
):
    slots, rows, columns = x_ref.shape
    for ref, dest in ((x_ref, tn_ref.at[0:rows]), (l_ref, tn_ref.at[rows : 2 * rows])):
        value = reordered(ref[...].reshape(slots * rows, columns))
        for slot in range(slots):
            interleave(lines_ref, slot, value[slot * rows : (slot + 1) * rows])
        copy_lines(lines_ref, dest)
    for kind, ref in enumerate((d_ref, z_ref, m_ref)):
        coef_ref[kind] = reordered(ref[...])
    parts = cells_ref.shape[2] // columns
    for kind, ref in enumerate((cells_ref, values_ref, weights_ref)):
        for slot in range(slots):
            for part in range(parts):
                tn_ref[2 * rows + kind * parts + part, slot : slot + 1, :] = ref[
                    slot, :, part * columns : (part + 1) * columns
                ].astype(jnp.float32)


def split(value, count=PIECES):
    pieces = []
    for _ in range(count):
        piece = value.astype(jnp.bfloat16).astype(jnp.float32)
        pieces.append(piece)
        value = value - piece
    return pieces


def scatter(observed, slots, row_ids, columns, w_lines, v_lines):
    rows, count = row_ids.shape
    column_ids = lax.broadcasted_iota(jnp.int32, (columns, count), 0)
    for slot in range(slots):
        cells, values, weights = observed(slot)
        row_of = cells // columns if columns & (columns - 1) else cells >> (columns.bit_length() - 1)
        column_of = cells - row_of * columns
        column_of = (column_of >> 1) + (column_of & 1) * (columns // 2)
        in_row = row_ids == row_of
        left = jnp.concatenate(
            [
                jnp.where(in_row, piece, 0.0).astype(jnp.bfloat16)
                for piece in split(weights) + split(weights * values)
            ],
            axis=0,
        )
        right = jnp.where(column_ids == column_of, 1.0, 0.0).astype(jnp.bfloat16)
        sums = lax.dot_general(
            left, right, (((1,), (1,)), ((), ())), preferred_element_type=jnp.float32
        )
        for lines, at in ((w_lines, 0), (v_lines, PIECES)):
            total = sums[at * rows : (at + 1) * rows]
            for piece in range(1, PIECES):
                total = total + sums[(at + piece) * rows : (at + piece + 1) * rows]
            interleave(lines, slot, total)
    for slot in range(slots, SUB):
        for lines in (w_lines, v_lines):
            interleave(lines, slot, jnp.zeros((rows, columns), jnp.float32))


def edge_kernel(
    xl_ref, coef_ref, cells_ref, values_ref, weights_ref,
    up_ref, dn_ref, du_ref, dd_ref, w_ref, v_ref, w_lines, v_lines,
):
    rows, columns = coef_ref.shape[1:]

    def observed(slot):
        return (cells_ref[slot], values_ref[slot], weights_ref[slot])

    lines = lax.broadcasted_iota(jnp.int32, (w_ref.shape[0], cells_ref.shape[2]), 0)
    row_ids = jnp.where(lines < DROWS, lines, lines + rows - 2 * DROWS)
    scatter(observed, SUB, row_ids, columns, w_lines, v_lines)
    copy_lines(w_lines, w_ref)
    copy_lines(v_lines, v_ref)
    for ref, diag, xs, ls, ds, ws in (
        (up_ref, du_ref, rows - MARGIN, rows - LROWS, rows - DROWS, DROWS),
        (dn_ref, dd_ref, 0, 0, 0, 0),
    ):
        for dest in (ref, diag):
            dest[0:MARGIN] = xl_ref[xs : xs + MARGIN]
            dest[MARGIN : MARGIN + LROWS] = xl_ref[rows + ls : rows + ls + LROWS]
            dest[MARGIN + LROWS : EDGE] = (
                w_ref[ws : ws + DROWS] * xl_ref[ds : ds + DROWS] - v_ref[ws : ws + DROWS]
            )
        for kind in range(3):
            flat = coef_ref[kind, xs : xs + MARGIN, :]
            for row in range(MARGIN):
                at = kind * MARGIN + row
                ref[EDGE + at // SUB, at % SUB : at % SUB + 1, :] = flat[row : row + 1]
        for at in range(3 * MARGIN, (ref.shape[0] - EDGE) * SUB):
            ref[EDGE + at // SUB, at % SUB : at % SUB + 1, :] = jnp.zeros((1, columns), jnp.float32)


def observation_kernel(
    tn_ref, cells_ref, values_ref, weights_ref, *refs
):
    fresh, (wa_ref, va_ref, wb_ref, vb_ref, lists_ref, w_lines, v_lines) = refs[:3], refs[3:]
    last = lax.axis_index("tm") == lax.axis_size("tm") - 1
    rows, _, columns = wa_ref.shape
    pltpu.sync_copy(tn_ref.at[2 * rows : 2 * rows + lists_ref.shape[0]], lists_ref)
    parts = lists_ref.shape[0] // 3
    fresh_slots = fresh[0].shape[0]
    row_ids = lax.broadcasted_iota(jnp.int32, (rows, cells_ref.shape[2]), 0)

    def own(slot):
        return (cells_ref[slot], values_ref[slot], weights_ref[slot])

    def following(slot):
        out = []
        for kind, ref in enumerate(fresh):
            moved = jnp.concatenate(
                [lists_ref[kind * parts + part, slot : slot + 1, :] for part in range(parts)], axis=1
            )
            moved = moved.astype(ref.dtype)
            if slot < fresh_slots:
                moved = jnp.where(last, ref[slot], moved)
            elif kind == 2:
                moved = jnp.where(last, 0.0, moved)
            out.append(moved)
        return out

    scatter(own, SUB, row_ids, columns, w_lines, v_lines)
    copy_lines(w_lines, wa_ref)
    copy_lines(v_lines, va_ref)
    scatter(following, SUB - 1, row_ids, columns, w_lines, v_lines)
    copy_lines(w_lines, wb_ref)
    copy_lines(v_lines, vb_ref)


def slot7(value):
    return jnp.broadcast_to(value[SUB - 1 : SUB], value.shape)


def widen_coefficients(flat_ref, cf_ref, total, row_of):
    rows_all = lax.axis_size("lat") * row_of[1]
    diff = flat_ref[0, 0:total, :]
    zonal = 0.5 * flat_ref[1, 0:total, :]
    merid = 0.5 * flat_ref[2, 0:total, :]
    row_global = lax.axis_index("lat") * row_of[1] + row_of[0](
        lax.broadcasted_iota(jnp.int32, diff.shape, 0)
    )
    inside = (row_global >= 0) & (row_global < rows_all)
    south = diff + merid
    north = diff - merid
    east = diff - zonal
    west = diff + zonal
    planes = (
        1.0 - 4.0 * diff,
        north,
        south,
        east,
        west,
        jnp.where(inside, rolled(south, -1, 0), 0.0),
        jnp.where(inside, rolled(north, 1, 0), 0.0),
        eastward(west),
        westward(east),
    )
    for index, plane in enumerate(planes):
        flat_ref[3 + index, 0:total, :] = plane

    def widen(step, carry):
        start = pl.multiple_of(step * SUB, SUB)
        for index in range(len(planes)):
            block = flat_ref[3 + index, pl.ds(start, SUB), :]
            for row in range(SUB):
                cf_ref[index, start + row] = jnp.broadcast_to(block[row : row + 1], block.shape)
        return carry

    lax.fori_loop(0, total // SUB, widen, 0)


def sweep(state, begin, stride, length, keep, frozen=None):
    xs_ref, ls_ref, ws_ref, vs_ref, p_ref, q_ref, cf_ref = state
    sub = sublane(xs_ref.shape[2:])

    def stencil(src, adjoint, depth, finish):
        base = 5 if adjoint else 1
        count = length - 2 * depth
        block = (count + 1) // 2
        offsets = list(range(count)) + list(range(stride, stride + count)) if stride else range(block)

        def step(index, carry):
            for row in offsets:
                at = begin + depth + index * block + row
                coef = [cf_ref[k, at] for k in (0, base, base + 1, base + 2, base + 3)]
                out = []
                for tile in range(2):
                    value = src[at, tile]
                    out.append(
                        coef[0] * value
                        + coef[1] * src[at + 1, tile]
                        + coef[2] * src[at - 1, tile]
                        + coef[3] * eastward(value)
                        + coef[4] * westward(value)
                    )
                finish(at, out)
            return carry

        if stride:
            step(0, 0)
        else:
            lax.fori_loop(0, 2, step, 0)

    def store(dest):
        def finish(at, out):
            dest[at, 0] = out[0]
            dest[at, 1] = out[1]

        return finish

    def forward_end(at, out):
        ahead_a = rolled(out[0], 1, 0)
        ahead_b = rolled(out[1], 1, 0)
        ahead_b = jnp.where(sub == 0, ahead_a, ahead_b)
        jump_a = jnp.where(sub == 0, 0.0, xs_ref[at, 0] - ahead_a)
        jump_b = xs_ref[at, 1] - ahead_b
        ls_ref[at, 0] = ls_ref[at, 0] + penalty_weight * jump_a
        ls_ref[at, 1] = jnp.where(keep, ls_ref[at, 1] + penalty_weight * jump_b, 0.0)

    def backward_end(at, out):
        back_a = rolled(out[0], -1, 0)
        back_b = rolled(out[1], -1, 0)
        back_a = jnp.where(sub == SUB - 1, back_b, back_a)
        for tile, after in ((0, back_a), (1, back_b)):
            value = xs_ref[at, tile]
            gradient = ws_ref[at, tile] * value - vs_ref[at, tile] + ls_ref[at, tile] - after
            new = value - step_size * gradient
            if frozen is not None and tile == 0:
                new = jnp.where(frozen, value, new)
            xs_ref[at, tile] = new

    stencil(xs_ref, False, 1, store(p_ref))
    stencil(p_ref, False, 2, store(q_ref))
    stencil(q_ref, False, 3, forward_end)
    stencil(ls_ref, True, 4, store(p_ref))
    stencil(p_ref, True, 5, store(q_ref))
    stencil(q_ref, True, 6, backward_end)


def time_ends():
    tm = lax.axis_index("tm")
    return tm == 0, tm == lax.axis_size("tm") - 1


def load_own(state, at, xl_ref, tn_ref, obs, first_row, count):
    xs_ref, ls_ref, ws_ref, vs_ref = state[:4]
    rows = obs[0].shape[0]
    for tile, ref in ((0, xl_ref), (1, tn_ref)):
        xs_ref[at : at + count, tile] = ref[first_row : first_row + count]
        ls_ref[at : at + count, tile] = ref[rows + first_row : rows + first_row + count]
        ws_ref[at : at + count, tile] = obs[2 * tile][first_row : first_row + count]
        vs_ref[at : at + count, tile] = obs[2 * tile + 1][first_row : first_row + count]


def outer_observations(state, at, rows_of):
    ws_ref, vs_ref = state[2:4]
    ws_ref[at : at + DROWS] = jnp.zeros((DROWS, *ws_ref.shape[1:]), jnp.float32)
    for row in range(DROWS):
        for tile in range(2):
            vs_ref[at + row, tile] = -rows_of(row, tile)


def strip_kernel(
    xl_ref, tn_ref, lo_ref, hi_ref, dlo_ref, dhi_ref, wa_ref, va_ref, wb_ref, vb_ref, coef_ref,
    x1_ref, l1_ref, x2_ref, l2_ref, up_ref, dn_ref, halo_ref, *state,
):
    state, flat_ref = state[:7], state[7]
    xs_ref, ls_ref, ws_ref, vs_ref, p_ref = state[:5]
    rows, _, columns = wa_ref.shape
    obs = (wa_ref, va_ref, wb_ref, vb_ref)
    _, last = time_ends()
    sub = sublane((SUB, columns))
    inner = STRIP - MARGIN
    total = 2 * STRIP
    for kind in range(3):
        for row in range(MARGIN):
            at = kind * MARGIN + row
            for base, ref in ((0, lo_ref), (MARGIN, hi_ref)):
                halo_ref[kind, base + row : base + row + 1, :] = ref[
                    EDGE + at // SUB, at % SUB : at % SUB + 1, :
                ]
        flat_ref[kind, 0:MARGIN, :] = halo_ref[kind, 0:MARGIN, :]
        flat_ref[kind, MARGIN:STRIP, :] = coef_ref[kind, 0:inner, :]
        flat_ref[kind, STRIP : STRIP + inner, :] = coef_ref[kind, rows - inner : rows, :]
        flat_ref[kind, STRIP + inner : total, :] = halo_ref[kind, MARGIN : 2 * MARGIN, :]
    widen_coefficients(
        flat_ref,
        state[6],
        total,
        (lambda at: jnp.where(at < STRIP, at - MARGIN, at - STRIP + rows - inner), rows),
    )
    load_own(state, MARGIN, xl_ref, tn_ref, obs, 0, MARGIN)
    load_own(state, STRIP + MARGIN, xl_ref, tn_ref, obs, rows - MARGIN, MARGIN)
    for refs, xat, lat_at, dat in (
        ((lo_ref, dlo_ref), 0, MARGIN - LROWS, MARGIN - DROWS),
        ((hi_ref, dhi_ref), STRIP + inner, STRIP + inner, STRIP + inner),
    ):
        for tile, ref in enumerate(refs):
            xs_ref[xat : xat + MARGIN, tile] = ref[0:MARGIN]
            ls_ref[lat_at : lat_at + LROWS, tile] = ref[MARGIN : MARGIN + LROWS]
        outer_observations(
            state, dat, lambda row, tile, refs=refs: refs[tile][MARGIN + LROWS + row]
        )
    keep = jnp.logical_not(last)
    sweep(state, 0, STRIP + MARGIN, 2 * MARGIN, keep)
    for dest, ref in ((xs_ref, x1_ref), (ls_ref, l1_ref)):
        count = ref.shape[0]
        dest[MARGIN + DROWS : 2 * MARGIN + DROWS] = ref[0:MARGIN]
        dest[STRIP + DROWS : STRIP + DROWS + MARGIN] = ref[count - MARGIN : count]
    sweep(state, DROWS, STRIP, 2 * MARGIN, keep)

    for ref, out, xat, lat_at, lpair, dat in (
        (dn_ref, 0, MARGIN, MARGIN, MARGIN, MARGIN),
        (
            up_ref,
            MARGIN,
            total - 2 * MARGIN,
            total - MARGIN - LROWS,
            total - MARGIN - 2 * ((LROWS + 1) // 2),
            total - MARGIN - DROWS,
        ),
    ):
        for row in range(MARGIN):
            at = xat + row
            xs_ref[at, 1] = jnp.where(last, slot7(xs_ref[at, 0]), xs_ref[at, 1])
        x2_ref[out : out + MARGIN] = xs_ref[xat : xat + MARGIN]
        l2_ref[out : out + MARGIN] = ls_ref[xat : xat + MARGIN]
        for row in range(DROWS):
            at = dat + row
            for tile in range(2):
                p_ref[at, tile] = ws_ref[at, tile] * xs_ref[at, tile] - vs_ref[at, tile]
        wide = narrow = 0
        for src, at, count, pair_at in (
            (xs_ref, xat, MARGIN, xat),
            (ls_ref, lat_at, LROWS, lpair),
            (p_ref, dat, DROWS, dat),
        ):
            for row in range(count):
                ref[wide + row] = jnp.where(sub < 2, src[at + row, 1], src[at + row, 0])
            wide += count
            for pair in range((count + 1) // 2):
                here = pair_at + 2 * pair
                ref[EDGE + narrow + pair] = two_rows(src[here, 1], src[here + 1, 1])
            narrow += (count + 1) // 2


def middle_kernel(
    xl_ref, tn_ref, wa_ref, va_ref, wb_ref, vb_ref, coef_ref, x1_ref, l1_ref, *state
):
    state, flat_ref = state[:7], state[7]
    xs_ref, ls_ref = state[:2]
    rows = wa_ref.shape[0]
    _, last = time_ends()
    for kind in range(3):
        flat_ref[kind, 0:rows, :] = coef_ref[kind]
    widen_coefficients(flat_ref, state[6], rows, (lambda at: at, rows))
    load_own(state, 0, xl_ref, tn_ref, (wa_ref, va_ref, wb_ref, vb_ref), 0, rows)
    sweep(state, 0, 0, rows, jnp.logical_not(last))
    x1_ref[...] = xs_ref[DROWS : rows - DROWS]
    l1_ref[...] = ls_ref[DROWS : rows - DROWS]


def inner_kernel(
    xstrip_ref, lstrip_ref, x1_ref, l1_ref, wa_ref, va_ref, wb_ref, vb_ref, coef_ref,
    x3_ref, l3_ref, *state,
):
    state, flat_ref = state[:7], state[7]
    xs_ref, ls_ref, ws_ref, vs_ref = state[:4]
    rows, _, columns = wa_ref.shape
    first, last = time_ends()
    sub = sublane((SUB, columns))
    for kind in range(3):
        flat_ref[kind, 0:rows, :] = coef_ref[kind]
    widen_coefficients(flat_ref, state[6], rows, (lambda at: at, rows))
    for tile, w, v in ((0, wa_ref, va_ref), (1, wb_ref, vb_ref)):
        ws_ref[0:rows, tile] = w[...]
        vs_ref[0:rows, tile] = v[...]
    xs_ref[DROWS : rows - DROWS] = x1_ref[...]
    ls_ref[DROWS : rows - DROWS] = l1_ref[...]
    sweep(state, DROWS, 0, rows - 2 * DROWS, jnp.logical_not(last))

    def fix(step, carry):
        at = MARGIN + step
        xs_ref[at, 1] = jnp.where(last, slot7(xs_ref[at, 0]), xs_ref[at, 1])
        return carry

    lax.fori_loop(0, rows - 2 * MARGIN, fix, 0, unroll=4)
    for dest, strip in ((xs_ref, xstrip_ref), (ls_ref, lstrip_ref)):
        dest[0:MARGIN] = strip[0:MARGIN]
        dest[rows - MARGIN : rows] = strip[MARGIN : 2 * MARGIN]
    sweep(state, 0, 0, rows, jnp.logical_not(last) | (sub < 4), first & (sub < 4))
    x3_ref[...] = xs_ref[DROWS : rows - DROWS]
    l3_ref[...] = ls_ref[DROWS : rows - DROWS]


def final_kernel(
    xstrip_ref, lstrip_ref, x3_ref, l3_ref, lo_ref, hi_ref, wa_ref, va_ref, wb_ref, vb_ref,
    coef_ref, halo_ref, xout_ref, lout_ref, *state,
):
    state, flat_ref, lines_ref = state[:7], state[7], state[8]
    xs_ref, ls_ref, ws_ref, vs_ref = state[:4]
    rows, _, columns = wa_ref.shape
    first, last = time_ends()
    top = MARGIN + rows
    sub = sublane((SUB, columns))
    for kind in range(3):
        flat_ref[kind, 0:MARGIN, :] = halo_ref[kind, 0:MARGIN, :]
        flat_ref[kind, MARGIN:top, :] = coef_ref[kind]
        flat_ref[kind, top : top + MARGIN, :] = halo_ref[kind, MARGIN : 2 * MARGIN, :]
    widen_coefficients(flat_ref, state[6], rows + 2 * MARGIN, (lambda at: at - MARGIN, rows))
    for dest, strip in ((xs_ref, xstrip_ref), (ls_ref, lstrip_ref)):
        dest[MARGIN : 2 * MARGIN] = strip[0:MARGIN]
        dest[top - MARGIN : top] = strip[MARGIN : 2 * MARGIN]
    for tile, w, v in ((0, wa_ref, va_ref), (1, wb_ref, vb_ref)):
        ws_ref[MARGIN:top, tile] = w[...]
        vs_ref[MARGIN:top, tile] = v[...]

    for ref, xat, lat_at, lskip, dat in (
        (lo_ref, 0, MARGIN - LROWS, LROWS % 2, MARGIN - DROWS),
        (hi_ref, top, top, 0, top),
    ):

        def outer(row, tile, wide, narrow, skip, ref=ref):
            own = ref[wide + row]
            if tile == 0:
                return own
            packed = ref[EDGE + narrow + (row + skip) // 2]
            if (row + skip) % 2:
                packed = rolled(packed, 4, 0)
            return jnp.where(sub < 2, own, packed)

        lpairs = MARGIN // 2
        for tile in range(2):
            for row in range(MARGIN):
                xs_ref[xat + row, tile] = outer(row, tile, 0, 0, 0)
            for row in range(LROWS):
                ls_ref[lat_at + row, tile] = outer(row, tile, MARGIN, lpairs, lskip)
        dpairs = lpairs + (LROWS + 1) // 2
        outer_observations(
            state,
            dat,
            lambda row, tile, outer=outer: outer(row, tile, MARGIN + LROWS, dpairs, 0),
        )
    keep = jnp.logical_not(last) | (sub < 4)
    sweep(state, 0, rows, 2 * MARGIN, keep, first & (sub < 4))
    xs_ref[MARGIN + DROWS : top - DROWS] = x3_ref[...]
    ls_ref[MARGIN + DROWS : top - DROWS] = l3_ref[...]
    sweep(state, DROWS, 0, rows + 2 * DROWS, keep)

    parts = columns // LANES
    for ref, dest in ((xs_ref, xout_ref), (ls_ref, lout_ref)):

        def gather(step, carry, ref=ref):
            value = jnp.where(
                sub < 4,
                rolled(ref[MARGIN + step, 0], 4, 0),
                rolled(ref[MARGIN + step, 1], 4, 0),
            )
            for part in range(parts):
                lines_ref[part, pl.ds(pl.multiple_of(step * SUB, SUB), SUB), :] = value[
                    :, part * LANES : (part + 1) * LANES
                ]
            return carry

        lax.fori_loop(0, rows, gather, 0, unroll=4)
        value = jnp.concatenate(
            [
                jnp.concatenate(
                    [lines_ref[part, pl.ds(slot, rows, stride=SUB), :] for part in range(parts)],
                    axis=1,
                )
                for slot in range(SUB)
            ],
            axis=0,
        )
        dest[...] = reordered(value, back=True).reshape(dest.shape)


def body(
    states,
    multipliers,
    diffusivity,
    zonal_speed,
    meridional_speed,
    observed_cells,
    observed_values,
    observed_weights,
    fresh_cells,
    fresh_values,
    fresh_weights,
):
    slots, rows, columns = states.shape
    tm_count, lat_count = lax.axis_size("tm"), lax.axis_size("lat")

    def send(value, tm_step, lat_step):
        pairs = []
        for t in range(tm_count):
            for b in range(lat_count):
                to_t, to_b = t + tm_step, b + lat_step
                if 0 <= to_t < tm_count and 0 <= to_b < lat_count:
                    pairs.append((t * lat_count + b, to_t * lat_count + to_b))
        return lax.ppermute(value, ("tm", "lat"), pairs)

    vmem = pl.BlockSpec(memory_space=pltpu.VMEM)

    def call(kernel, outs, args, scratch=(), hbm=()):
        specs = [vmem] * len(args)
        for index in hbm:
            specs[index] = pl.BlockSpec(memory_space=pl.ANY)
        return pl.pallas_call(
            kernel,
            out_shape=[jax.ShapeDtypeStruct(shape, jnp.float32) for shape in outs],
            in_specs=specs,
            out_specs=[vmem] * len(outs),
            scratch_shapes=list(scratch),
        )(*args)

    tile = (SUB, columns)
    lines = pltpu.VMEM((columns // LANES, rows * SUB, LANES), jnp.float32)
    field = (rows, *tile)
    lists = 3 * (observed_cells.shape[-1] // columns)
    coef_rows = -(-3 * MARGIN // SUB)

    def state(length):
        return (
            [pltpu.VMEM((length + 2, 2, *tile), jnp.float32)] * 6
            + [pltpu.VMEM((9, length + 2, *tile), jnp.float32)]
            + [pltpu.VMEM((12, length, columns), jnp.float32)]
        )

    obs = (observed_cells, observed_values, observed_weights)
    xl, coef = call(
        prep_kernel,
        ((2 * rows + lists, *tile), (3, rows, columns)),
        (states, multipliers, diffusivity, zonal_speed, meridional_speed, *obs),
        (lines,),
    )
    tn = send(xl, -1, 0)
    edge_rows = -(-2 * DROWS // 16) * 16
    edge_lines = pltpu.VMEM((columns // LANES, edge_rows * SUB, LANES), jnp.float32)
    up, dn, du, dd = call(
        edge_kernel,
        ([(EDGE + coef_rows, *tile)] * 2 + [(EDGE, *tile)] * 2),
        (xl, coef, *obs),
        [pltpu.VMEM((edge_rows, *tile), jnp.float32)] * 2 + [edge_lines] * 2,
    )
    lo = send(up, 0, 1)
    hi = send(dn, 0, -1)
    dlo = send(du, -1, 1)
    dhi = send(dd, -1, -1)
    obs = call(
        observation_kernel,
        (field, field, field, field),
        (tn, *obs, fresh_cells, fresh_values, fresh_weights),
        (pltpu.VMEM((lists, *tile), jnp.float32), lines, lines),
        hbm=(0,),
    )
    outer = (2 * MARGIN, 2, *tile)
    inner = (rows - 2 * DROWS, 2, *tile)
    x1, l1 = call(middle_kernel, (inner, inner), (xl, tn, *obs, coef), state(rows))
    xstrip, lstrip, up, dn, halo = call(
        strip_kernel,
        (outer, outer, *[(EDGE + PAIRS, *tile)] * 2, (3, 2 * MARGIN, columns)),
        (xl, tn, lo, hi, dlo, dhi, *obs, coef, x1, l1),
        state(2 * STRIP),
    )
    lo = send(up, 0, 1)
    hi = send(dn, 0, -1)
    x3, l3 = call(
        inner_kernel, (inner, inner), (xstrip, lstrip, x1, l1, *obs, coef), state(rows)
    )
    return tuple(
        call(
            final_kernel,
            (states.shape, states.shape),
            (xstrip, lstrip, x3, l3, lo, hi, *obs, coef, halo),
            state(rows + 2 * MARGIN) + [lines],
        )
    )


def solution(mesh):
    in_specs = (
        P("tm", "lat", None),
        P("tm", "lat", None),
        P("lat", None),
        P("lat", None),
        P("lat", None),
        P("tm", "lat", None),
        P("tm", "lat", None),
        P("tm", "lat", None),
        P(None, "lat", None),
        P(None, "lat", None),
        P(None, "lat", None),
    )
    out_specs = (P("tm", "lat", None), P("tm", "lat", None))
    return jax.shard_map(body, mesh=mesh, in_specs=in_specs, out_specs=out_specs, check_vma=False)
```

time: 83.7 us -> 76.6 us (0.915)
  the two profiles are of different devices: /device:TPU:16 before, /device:TPU:27 now
where the time goes in v1:
time: 76.6 us; the launch traced here: 76.2 us
  Pallas kernels  47 us (61%)
  starting transfers between devices  21.5 us (28%)
  waiting for transfers between devices  4.24 us (6%)
  local copies, waits for them, and re-layouts  2.64 us (3%)
    pallas_call x7, Pallas kernels, call(): pl.pallas_call(kernel, out_shape=[jax.ShapeDtypeStruct(shape, jnp.float32...  47 us
    ppermute x7, starting transfers between devices, send(): return lax.ppermute(value, ('tm', 'lat'), pairs)  21.5 us
    ppermute x7, waiting for transfers between devices, send(): return lax.ppermute(value, ('tm', 'lat'), pairs)  4.24 us
    unnamed x14, local copies, waits for them, and re-layouts  2.64 us
  transfers between devices with their start and end apart: 7, of which 1 were waited for; matrix products, arithmetic and copies ran while one was open for 0% of the time, Pallas kernels for 35%

profile of v1, /device:TPU:27, one launch (start us, length us, event | category | flops | bytes accessed | tf_op | source)
XLA Modules:
  0.0 76.2 jit_solution(14695298609317522170)
XLA Ops:
  0.6 3.2 %shard_map.122 = (f32[140,8,256]{2,1,0:T(8,128)}, f32[3,64,256]{2,1,0:T(8,128)}) custom-call(f32[8,64,256]{2,1,0:T(8,128)} %x_ref.1, f32[8,64,256]{2,1,0:T(8,128)} %l_ref.1, f32[64,256]{1,0:T(8,128)} %d_ref.1, f32[64,256]{1,0:T(8,128)} %z_ref.1, f32[64,256]{1,0:T(8,128)} %m_ref.1, s32[8,1,1024]{2,1,0:T(1,128)} %cells_ref.5, f32[8,1,1024]{2,1,0:T(1,128)} %values_ref.5, ...), custom_call_target="tpu_custom_call" | custom-call | tf_op jit(solution)/shard_map/pallas_call | solution.py:581
  3.8 2.6 %collective-permute-start = (f32[140,8,256]{2,1,0:T(8,128)}, f32[140,8,256]{2,1,0:T(8,128)S(1)}, u32[]{:S(2)}, u32[]{:S(2)}) collective-permute-start(f32[140,8,256]{2,1,0:T(8,128)} %get-tuple-element.21.xl_ref), channel_id=1, source_target_pairs={{8,0},{9,1},{10,2},{11,3},{12,4},{13,5},{14,6},{15,7},{16,8},{17,9... | collective-permute-start | bytes 3440648 | tf_op jit(solution)/shard_map/ppermute | solution.py:573
  6.5 3.8 %shard_map.123 = (f32[32,8,256]{2,1,0:T(8,128)}, f32[32,8,256]{2,1,0:T(8,128)}, f32[27,8,256]{2,1,0:T(8,128)}, f32[27,8,256]{2,1,0:T(8,128)}) custom-call(f32[140,8,256]{2,1,0:T(8,128)} %get-tuple-element.21.xl_ref, f32[3,64,256]{2,1,0:T(8,128)} %get-tuple-element.22.coef_ref, s32[8,1,1024]{2,1,0:T(1,128)} %cells_ref.5, f32[8,1,1024]{2,1,0:T(1,128)} %values_ref.5, ...), custom_call_target="tpu_custom_call" | custom-call | tf_op jit(solution)/shard_map/pallas_call | solution.py:581
  10.3 3.1 %collective-permute-start.1 = (f32[32,8,256]{2,1,0:T(8,128)}, f32[32,8,256]{2,1,0:T(8,128)S(1)}, u32[]{:S(2)}, u32[]{:S(2)}) collective-permute-start(f32[32,8,256]{2,1,0:T(8,128)} %get-tuple-element.23), channel_id=1, source_target_pairs={{0,1},{1,2},{2,3},{3,4},{4,5},{5,6},{6,7},{8,9},{9,10},{10,11},{11... | collective-permute-start | bytes 786440 | tf_op jit(solution)/shard_map/ppermute | solution.py:573
  13.5 3.0 %collective-permute-start.2 = (f32[32,8,256]{2,1,0:T(8,128)}, f32[32,8,256]{2,1,0:T(8,128)S(1)}, u32[]{:S(2)}, u32[]{:S(2)}) collective-permute-start(f32[32,8,256]{2,1,0:T(8,128)} %get-tuple-element.24), channel_id=1, source_target_pairs={{1,0},{2,1},{3,2},{4,3},{5,4},{6,5},{7,6},{9,8},{10,9},{11,10},{12... | collective-permute-start | bytes 786440 | tf_op jit(solution)/shard_map/ppermute | solution.py:573
  16.5 2.7 %collective-permute-start.3 = (f32[27,8,256]{2,1,0:T(8,128)}, f32[27,8,256]{2,1,0:T(8,128)S(1)}, u32[]{:S(2)}, u32[]{:S(2)}) collective-permute-start(f32[27,8,256]{2,1,0:T(8,128)} %get-tuple-element.25), channel_id=1, source_target_pairs={{8,1},{9,2},{10,3},{11,4},{12,5},{13,6},{14,7},{16,9},{17,10},{18,... | collective-permute-start | bytes 663560 | tf_op jit(solution)/shard_map/ppermute | solution.py:573
  19.2 3.7 %collective-permute-start.4 = (f32[27,8,256]{2,1,0:T(8,128)}, f32[27,8,256]{2,1,0:T(8,128)S(1)}, u32[]{:S(2)}, u32[]{:S(2)}) collective-permute-start(f32[27,8,256]{2,1,0:T(8,128)} %get-tuple-element.26), channel_id=1, source_target_pairs={{9,0},{10,1},{11,2},{12,3},{13,4},{14,5},{15,6},{17,8},{18,9},{19,... | collective-permute-start | bytes 663560 | tf_op jit(solution)/shard_map/ppermute | solution.py:573
  22.9 0.0 collective-permute-done.tn_ref
  22.9 0.0 copy-start
  22.9 1.0 %copy-done = f32[140,8,256]{2,1,0:T(8,128)} copy-done((f32[140,8,256]{2,1,0:T(8,128)}, f32[140,8,256]{2,1,0:T(8,128)S(1)}, u32[]{:S(2)}) %copy-start) | copy-done | bytes 1146904
  23.9 6.2 %shard_map.124 = (f32[64,8,256]{2,1,0:T(8,128)}, f32[64,8,256]{2,1,0:T(8,128)}, f32[64,8,256]{2,1,0:T(8,128)}, f32[64,8,256]{2,1,0:T(8,128)}) custom-call(f32[140,8,256]{2,1,0:T(8,128)} %copy-done, s32[8,1,1024]{2,1,0:T(1,128)} %cells_ref.5, f32[8,1,1024]{2,1,0:T(1,128)} %values_ref.5, f32[8,1,1024]{2,1,0:T(1,128)} %weights_ref.5, s32[4,1,1024]{2,1,0:T(1,128)} %refs_0_.1, ...), custom_call_target="tpu_custom_call" | custom-call | tf_op jit(solution)/shard_map/pallas_call | solution.py:581
  30.1 7.0 %shard_map.125 = (f32[52,2,8,256]{3,2,1,0:T(8,128)}, f32[52,2,8,256]{3,2,1,0:T(8,128)}) custom-call(f32[140,8,256]{2,1,0:T(8,128)} %get-tuple-element.21.xl_ref, f32[140,8,256]{2,1,0:T(8,128)} %copy-done, f32[64,8,256]{2,1,0:T(8,128)} %get-tuple-element.27.wa_ref, f32[64,8,256]{2,1,0:T(8,128)} %get-tuple-element.28.va_ref, ...), custom_call_target="tpu_custom_call" | custom-call | tf_op jit(solution)/shard_map/pallas_call | solution.py:581
  37.1 0.0 collective-permute-done.3.dlo_ref
  37.1 0.0 collective-permute-done.4.dhi_ref
  37.1 0.0 copy-start.6
  37.1 0.0 collective-permute-done.1.lo_ref
  37.1 0.0 copy-start.3
  37.1 0.0 collective-permute-done.2.hi_ref
  37.2 0.0 copy-start.4
  37.2 0.6 copy-done.5
  37.8 0.1 copy-done.6
  37.9 0.1 copy-done.3
  38.0 0.1 copy-done.4
  38.1 7.1 %shard_map.126 = (f32[24,2,8,256]{3,2,1,0:T(8,128)}, f32[24,2,8,256]{3,2,1,0:T(8,128)}, f32[41,8,256]{2,1,0:T(8,128)}, f32[41,8,256]{2,1,0:T(8,128)}, f32[3,24,256]{2,1,0:T(8,128)}) custom-call(f32[140,8,256]{2,1,0:T(8,128)} %get-tuple-element.21.xl_ref, f32[140,8,256]{2,1,0:T(8,128)} %copy-done, f32[32,8,256]{2,1,0:T(8,128)} %copy-done.3, ...), custom_call_target="tpu_custom_call" | custom-call | tf_op jit(solution)/shard_map/pallas_call | solution.py:581
  45.1 1.9 %collective-permute-start.5 = (f32[41,8,256]{2,1,0:T(8,128)}, f32[41,8,256]{2,1,0:T(8,128)S(1)}, u32[]{:S(2)}, u32[]{:S(2)}) collective-permute-start(f32[41,8,256]{2,1,0:T(8,128)} %get-tuple-element.37), channel_id=1, source_target_pairs={{0,1},{1,2},{2,3},{3,4},{4,5},{5,6},{6,7},{8,9},{9,10},{10,11},{11... | collective-permute-start | bytes 1007624 | tf_op jit(solution)/shard_map/ppermute | solution.py:573
  47.0 4.4 %collective-permute-start.6 = (f32[41,8,256]{2,1,0:T(8,128)}, f32[41,8,256]{2,1,0:T(8,128)S(1)}, u32[]{:S(2)}, u32[]{:S(2)}) collective-permute-start(f32[41,8,256]{2,1,0:T(8,128)} %get-tuple-element.38), channel_id=1, source_target_pairs={{1,0},{2,1},{3,2},{4,3},{5,4},{6,5},{7,6},{9,8},{10,9},{11,10},{12... | collective-permute-start | bytes 1007624 | tf_op jit(solution)/shard_map/ppermute | solution.py:573
  51.5 9.5 %shard_map.127 = (f32[52,2,8,256]{3,2,1,0:T(8,128)}, f32[52,2,8,256]{3,2,1,0:T(8,128)}) custom-call(f32[24,2,8,256]{3,2,1,0:T(8,128)} %get-tuple-element.33.xstrip_ref, f32[24,2,8,256]{3,2,1,0:T(8,128)} %get-tuple-element.34.lstrip_ref, f32[52,2,8,256]{3,2,1,0:T(8,128)} %get-tuple-element.31.x1_ref, f32[52,2,8,256]{3,2,1,0:T(8,128)} %get-tuple-element.32.l1_ref, ...), custom_call_target="tpu_custom_call" | custom-call | tf_op jit(solution)/shard_map/pallas_call | solution.py:581
  61.0 0.0 collective-permute-done.5.lo_ref
  61.0 4.2 %collective-permute-done.6.hi_ref = f32[41,8,256]{2,1,0:T(8,128)S(1)} collective-permute-done((f32[41,8,256]{2,1,0:T(8,128)}, f32[41,8,256]{2,1,0:T(8,128)S(1)}, u32[]{:S(2)}, u32[]{:S(2)}) %collective-permute-start.6) | collective-permute-done | bytes 335904 | tf_op jit(solution)/shard_map/ppermute | solution.py:573
  65.2 0.0 copy-done.1
  65.2 0.7 copy-done.2
  65.9 10.3 %shard_map.128 = (f32[8,64,256]{2,1,0:T(8,128)}, f32[8,64,256]{2,1,0:T(8,128)}) custom-call(f32[24,2,8,256]{3,2,1,0:T(8,128)} %get-tuple-element.33.xstrip_ref, f32[24,2,8,256]{3,2,1,0:T(8,128)} %get-tuple-element.34.lstrip_ref, f32[52,2,8,256]{3,2,1,0:T(8,128)} %get-tuple-element.35.x3_ref, f32[52,2,8,256]{3,2,1,0:T(8,128)} %get-tuple-element.36.l3_ref, ...), custom_call_target="tpu_custom_call" | custom-call | tf_op jit(solution)/shard_map/pallas_call | solution.py:581
  (3 shorter events, 0.0 us)
Async XLA Ops:
  3.8 19.1 %collective-permute-start = (f32[140,8,256]{2,1,0:T(8,128)}, f32[140,8,256]{2,1,0:T(8,128)S(1)}, u32[]{:S(2)}, u32[]{:S(2)}) collective-permute-start(f32[140,8,256]{2,1,0:T(8,128)} %get-tuple-element.21.xl_ref), channel_id=1, source_target_pairs={{8,0},{9,1},{10,2},{11,3},{12,4},{13,5},{14,6},{15,7},{16,8},{17,9... | collective-permute-start | bytes 3440648 | tf_op jit(solution)/shard_map/ppermute | solution.py:573
  10.3 26.8 %collective-permute-start.1 = (f32[32,8,256]{2,1,0:T(8,128)}, f32[32,8,256]{2,1,0:T(8,128)S(1)}, u32[]{:S(2)}, u32[]{:S(2)}) collective-permute-start(f32[32,8,256]{2,1,0:T(8,128)} %get-tuple-element.23), channel_id=1, source_target_pairs={{0,1},{1,2},{2,3},{3,4},{4,5},{5,6},{6,7},{8,9},{9,10},{10,11},{11... | collective-permute-start | bytes 786440 | tf_op jit(solution)/shard_map/ppermute | solution.py:573
  13.5 23.7 %collective-permute-start.2 = (f32[32,8,256]{2,1,0:T(8,128)}, f32[32,8,256]{2,1,0:T(8,128)S(1)}, u32[]{:S(2)}, u32[]{:S(2)}) collective-permute-start(f32[32,8,256]{2,1,0:T(8,128)} %get-tuple-element.24), channel_id=1, source_target_pairs={{1,0},{2,1},{3,2},{4,3},{5,4},{6,5},{7,6},{9,8},{10,9},{11,10},{12... | collective-permute-start | bytes 786440 | tf_op jit(solution)/shard_map/ppermute | solution.py:573
  16.5 20.6 %collective-permute-start.3 = (f32[27,8,256]{2,1,0:T(8,128)}, f32[27,8,256]{2,1,0:T(8,128)S(1)}, u32[]{:S(2)}, u32[]{:S(2)}) collective-permute-start(f32[27,8,256]{2,1,0:T(8,128)} %get-tuple-element.25), channel_id=1, source_target_pairs={{8,1},{9,2},{10,3},{11,4},{12,5},{13,6},{14,7},{16,9},{17,10},{18,... | collective-permute-start | bytes 663560 | tf_op jit(solution)/shard_map/ppermute | solution.py:573
  19.2 17.9 %collective-permute-start.4 = (f32[27,8,256]{2,1,0:T(8,128)}, f32[27,8,256]{2,1,0:T(8,128)S(1)}, u32[]{:S(2)}, u32[]{:S(2)}) collective-permute-start(f32[27,8,256]{2,1,0:T(8,128)} %get-tuple-element.26), channel_id=1, source_target_pairs={{9,0},{10,1},{11,2},{12,3},{13,4},{14,5},{15,6},{17,8},{18,9},{19,... | collective-permute-start | bytes 663560 | tf_op jit(solution)/shard_map/ppermute | solution.py:573
  22.9 1.0 %copy-start = (f32[140,8,256]{2,1,0:T(8,128)}, f32[140,8,256]{2,1,0:T(8,128)S(1)}, u32[]{:S(2)}) copy-start(f32[140,8,256]{2,1,0:T(8,128)S(1)} %collective-permute-done.tn_ref) | copy-start | bytes 3440644
  37.1 0.7 copy-start.5
  37.1 0.8 copy-start.6
  37.1 0.8 %copy-start.3 = (f32[32,8,256]{2,1,0:T(8,128)}, f32[32,8,256]{2,1,0:T(8,128)S(1)}, u32[]{:S(2)}) copy-start(f32[32,8,256]{2,1,0:T(8,128)S(1)} %collective-permute-done.1.lo_ref) | copy-start | bytes 786436
  37.2 0.9 %copy-start.4 = (f32[32,8,256]{2,1,0:T(8,128)}, f32[32,8,256]{2,1,0:T(8,128)S(1)}, u32[]{:S(2)}) copy-start(f32[32,8,256]{2,1,0:T(8,128)S(1)} %collective-permute-done.2.hi_ref) | copy-start | bytes 786436
  45.1 15.8 %collective-permute-start.5 = (f32[41,8,256]{2,1,0:T(8,128)}, f32[41,8,256]{2,1,0:T(8,128)S(1)}, u32[]{:S(2)}, u32[]{:S(2)}) collective-permute-start(f32[41,8,256]{2,1,0:T(8,128)} %get-tuple-element.37), channel_id=1, source_target_pairs={{0,1},{1,2},{2,3},{3,4},{4,5},{5,6},{6,7},{8,9},{9,10},{10,11},{11... | collective-permute-start | bytes 1007624 | tf_op jit(solution)/shard_map/ppermute | solution.py:573
  47.0 18.1 %collective-permute-start.6 = (f32[41,8,256]{2,1,0:T(8,128)}, f32[41,8,256]{2,1,0:T(8,128)S(1)}, u32[]{:S(2)}, u32[]{:S(2)}) collective-permute-start(f32[41,8,256]{2,1,0:T(8,128)} %get-tuple-element.38), channel_id=1, source_target_pairs={{1,0},{2,1},{3,2},{4,3},{5,4},{6,5},{7,6},{9,8},{10,9},{11,10},{12... | collective-permute-start | bytes 1007624 | tf_op jit(solution)/shard_map/ppermute | solution.py:573
  61.0 4.2 %copy-start.1 = (f32[41,8,256]{2,1,0:T(8,128)}, f32[41,8,256]{2,1,0:T(8,128)S(1)}, u32[]{:S(2)}) copy-start(f32[41,8,256]{2,1,0:T(8,128)S(1)} %collective-permute-done.5.lo_ref) | copy-start | bytes 1007620
  65.2 0.7 copy-start.2

commit v2 on v1

--- a/solution.py
+++ b/solution.py
@@ -16,7 +16,7 @@
 PAIRS = MARGIN // 2 + (LROWS + 1) // 2 + DROWS // 2
 STRIP = 3 * MARGIN
 LANES = 128
-PIECES = 3
+PIECES = 2
 
 
 def rolled(value, shift, axis):
@@ -30,6 +30,16 @@
 def two_rows(first, second):
     sub = sublane(first.shape)
     return jnp.where((sub >= 2) & (sub < 6), first, rolled(second, 4, 0))
+
+
+def started(pairs, sem_ref):
+    copies = [
+        pltpu.make_async_copy(source, dest, sem_ref.at[index])
+        for index, (source, dest) in enumerate(pairs)
+    ]
+    for copy in copies:
+        copy.start()
+    return copies
 
 
 def eastward(value):
@@ -101,21 +111,32 @@
 
 def scatter(observed, slots, row_ids, columns, w_lines, v_lines):
     rows, count = row_ids.shape
-    column_ids = lax.broadcasted_iota(jnp.int32, (columns, count), 0)
+    kind = jnp.bfloat16 if columns <= 256 else jnp.float32
+    group = (rows // 16, 16, count)
+    rows_named = row_ids.astype(jnp.float32).reshape(group).astype(kind)
+    columns_named = lax.broadcasted_iota(jnp.int32, (columns, count), 0).astype(jnp.float32)
+    columns_named = columns_named.reshape(columns // 16, 16, count).astype(kind)
+    zero = jnp.zeros((), jnp.bfloat16)
+    one = jnp.ones((1, 16, count), jnp.bfloat16)
+
+    def spread(line, dtype):
+        return jnp.broadcast_to(line.astype(jnp.float32), (16, count)).astype(dtype)[None]
+
     for slot in range(slots):
         cells, values, weights = observed(slot)
         row_of = cells // columns if columns & (columns - 1) else cells >> (columns.bit_length() - 1)
         column_of = cells - row_of * columns
         column_of = (column_of >> 1) + (column_of & 1) * (columns // 2)
-        in_row = row_ids == row_of
+        in_row = rows_named == spread(row_of, kind)
         left = jnp.concatenate(
             [
-                jnp.where(in_row, piece, 0.0).astype(jnp.bfloat16)
+                jnp.where(in_row, spread(piece, jnp.bfloat16), zero).reshape(rows, count)
                 for piece in split(weights) + split(weights * values)
             ],
             axis=0,
         )
-        right = jnp.where(column_ids == column_of, 1.0, 0.0).astype(jnp.bfloat16)
+        right = jnp.where(columns_named == spread(column_of, kind), one, zero)
+        right = right.reshape(columns, count)
         sums = lax.dot_general(
             left, right, (((1,), (1,)), ((), ())), preferred_element_type=jnp.float32
         )
@@ -131,9 +152,17 @@
 
 def edge_kernel(
     xl_ref, coef_ref, cells_ref, values_ref, weights_ref,
-    up_ref, dn_ref, du_ref, dd_ref, w_ref, v_ref, w_lines, v_lines,
+    up_ref, dn_ref, du_ref, dd_ref, w_ref, v_ref, w_lines, v_lines, x_ref, l_ref, sem_ref,
 ):
     rows, columns = coef_ref.shape[1:]
+    copies = started(
+        [
+            (xl_ref.at[base + at : base + at + MARGIN], ref.at[out : out + MARGIN])
+            for base, ref in ((0, x_ref), (rows, l_ref))
+            for at, out in ((0, 0), (rows - MARGIN, MARGIN))
+        ],
+        sem_ref,
+    )
 
     def observed(slot):
         return (cells_ref[slot], values_ref[slot], weights_ref[slot])
@@ -143,15 +172,17 @@
     scatter(observed, SUB, row_ids, columns, w_lines, v_lines)
     copy_lines(w_lines, w_ref)
     copy_lines(v_lines, v_ref)
-    for ref, diag, xs, ls, ds, ws in (
-        (up_ref, du_ref, rows - MARGIN, rows - LROWS, rows - DROWS, DROWS),
-        (dn_ref, dd_ref, 0, 0, 0, 0),
+    for copy in copies:
+        copy.wait()
+    for ref, diag, xs, out, ls, ds, ws in (
+        (up_ref, du_ref, rows - MARGIN, MARGIN, 2 * MARGIN - LROWS, 2 * MARGIN - DROWS, DROWS),
+        (dn_ref, dd_ref, 0, 0, 0, 0, 0),
     ):
         for dest in (ref, diag):
-            dest[0:MARGIN] = xl_ref[xs : xs + MARGIN]
-            dest[MARGIN : MARGIN + LROWS] = xl_ref[rows + ls : rows + ls + LROWS]
+            dest[0:MARGIN] = x_ref[out : out + MARGIN]
+            dest[MARGIN : MARGIN + LROWS] = l_ref[ls : ls + LROWS]
             dest[MARGIN + LROWS : EDGE] = (
-                w_ref[ws : ws + DROWS] * xl_ref[ds : ds + DROWS] - v_ref[ws : ws + DROWS]
+                v_ref[ws : ws + DROWS] - w_ref[ws : ws + DROWS] * x_ref[ds : ds + DROWS]
             )
         for kind in range(3):
             flat = coef_ref[kind, xs : xs + MARGIN, :]
@@ -198,11 +229,15 @@
     copy_lines(v_lines, vb_ref)
 
 
+def middle_slots(first, second):
+    return jnp.where(sublane(first.shape) < 4, rolled(first, 4, 0), rolled(second, 4, 0))
+
+
 def slot7(value):
     return jnp.broadcast_to(value[SUB - 1 : SUB], value.shape)
 
 
-def widen_coefficients(flat_ref, cf_ref, total, row_of):
+def fold_coefficients(flat_ref, total, row_of):
     rows_all = lax.axis_size("lat") * row_of[1]
     diff = flat_ref[0, 0:total, :]
     zonal = 0.5 * flat_ref[1, 0:total, :]
@@ -229,53 +264,36 @@
     for index, plane in enumerate(planes):
         flat_ref[3 + index, 0:total, :] = plane
 
-    def widen(step, carry):
-        start = pl.multiple_of(step * SUB, SUB)
-        for index in range(len(planes)):
-            block = flat_ref[3 + index, pl.ds(start, SUB), :]
-            for row in range(SUB):
-                cf_ref[index, start + row] = jnp.broadcast_to(block[row : row + 1], block.shape)
-        return carry
-
-    lax.fori_loop(0, total // SUB, widen, 0)
-
-
-def sweep(state, begin, stride, length, keep, frozen=None):
-    xs_ref, ls_ref, ws_ref, vs_ref, p_ref, q_ref, cf_ref = state
+
+def sweep(state, begin, stride, length, keep, frozen=None, emit=None):
+    xs_ref, ls_ref, ws_ref, vs_ref, p_ref, q_ref, flat_ref = state
     sub = sublane(xs_ref.shape[2:])
 
-    def stencil(src, adjoint, depth, finish):
+    def stencil(src, adjoint, depth, finish, tiles=2):
         base = 5 if adjoint else 1
         count = length - 2 * depth
-        block = (count + 1) // 2
-        offsets = list(range(count)) + list(range(stride, stride + count)) if stride else range(block)
-
-        def step(index, carry):
-            for row in offsets:
-                at = begin + depth + index * block + row
-                coef = [cf_ref[k, at] for k in (0, base, base + 1, base + 2, base + 3)]
-                out = []
-                for tile in range(2):
-                    value = src[at, tile]
-                    out.append(
-                        coef[0] * value
-                        + coef[1] * src[at + 1, tile]
-                        + coef[2] * src[at - 1, tile]
-                        + coef[3] * eastward(value)
-                        + coef[4] * westward(value)
-                    )
-                finish(at, out)
-            return carry
-
-        if stride:
-            step(0, 0)
-        else:
-            lax.fori_loop(0, 2, step, 0)
+        for row in list(range(count)) + (list(range(stride, stride + count)) if stride else []):
+            at = begin + depth + row
+            coef = [
+                jnp.broadcast_to(flat_ref[3 + k, at : at + 1, :], xs_ref.shape[2:])
+                for k in (0, base, base + 1, base + 2, base + 3)
+            ]
+            out = []
+            for tile in range(tiles):
+                value = src[at, tile]
+                out.append(
+                    coef[0] * value
+                    + coef[1] * src[at + 1, tile]
+                    + coef[2] * src[at - 1, tile]
+                    + coef[3] * eastward(value)
+                    + coef[4] * westward(value)
+                )
+            finish(at, out)
 
     def store(dest):
         def finish(at, out):
-            dest[at, 0] = out[0]
-            dest[at, 1] = out[1]
+            for tile, value in enumerate(out):
+                dest[at, tile] = value
 
         return finish
 
@@ -285,8 +303,15 @@
         ahead_b = jnp.where(sub == 0, ahead_a, ahead_b)
         jump_a = jnp.where(sub == 0, 0.0, xs_ref[at, 0] - ahead_a)
         jump_b = xs_ref[at, 1] - ahead_b
-        ls_ref[at, 0] = ls_ref[at, 0] + penalty_weight * jump_a
-        ls_ref[at, 1] = jnp.where(keep, ls_ref[at, 1] + penalty_weight * jump_b, 0.0)
+        new_a = ls_ref[at, 0] + penalty_weight * jump_a
+        new_b = jnp.where(keep, ls_ref[at, 1] + penalty_weight * jump_b, 0.0)
+        if emit is not None:
+            ls_ref[at, 1] = middle_slots(new_a, new_b)
+            new_a = jnp.where(sub < 3, rolled(new_a, -5, 0), rolled(new_b, 3, 0))
+            new_b = None
+        ls_ref[at, 0] = new_a
+        if new_b is not None:
+            ls_ref[at, 1] = new_b
 
     def backward_end(at, out):
         back_a = rolled(out[0], -1, 0)
@@ -300,12 +325,18 @@
                 new = jnp.where(frozen, value, new)
             xs_ref[at, tile] = new
 
+    def emit_end(at, out):
+        value, w, v = (middle_slots(ref[at, 0], ref[at, 1]) for ref in (xs_ref, ws_ref, vs_ref))
+        lagrange = ls_ref[at, 1]
+        emit(at, value - step_size * (w * value - v + lagrange - out[0]), lagrange)
+
+    tiles = 2 if emit is None else 1
     stencil(xs_ref, False, 1, store(p_ref))
     stencil(p_ref, False, 2, store(q_ref))
     stencil(q_ref, False, 3, forward_end)
-    stencil(ls_ref, True, 4, store(p_ref))
-    stencil(p_ref, True, 5, store(q_ref))
-    stencil(q_ref, True, 6, backward_end)
+    stencil(ls_ref, True, 4, store(p_ref), tiles)
+    stencil(p_ref, True, 5, store(q_ref), tiles)
+    stencil(q_ref, True, 6, backward_end if emit is None else emit_end, tiles)
 
 
 def time_ends():
@@ -313,14 +344,19 @@
     return tm == 0, tm == lax.axis_size("tm") - 1
 
 
-def load_own(state, at, xl_ref, tn_ref, obs, first_row, count):
+def own_copies(state, at, xl_ref, tn_ref, obs, first_row, count):
     xs_ref, ls_ref, ws_ref, vs_ref = state[:4]
     rows = obs[0].shape[0]
+    pairs = []
     for tile, ref in ((0, xl_ref), (1, tn_ref)):
-        xs_ref[at : at + count, tile] = ref[first_row : first_row + count]
-        ls_ref[at : at + count, tile] = ref[rows + first_row : rows + first_row + count]
-        ws_ref[at : at + count, tile] = obs[2 * tile][first_row : first_row + count]
-        vs_ref[at : at + count, tile] = obs[2 * tile + 1][first_row : first_row + count]
+        for dest, source, start in (
+            (xs_ref, ref, first_row),
+            (ls_ref, ref, rows + first_row),
+            (ws_ref, obs[2 * tile], first_row),
+            (vs_ref, obs[2 * tile + 1], first_row),
+        ):
+            pairs.append((source.at[start : start + count], dest.at[at : at + count, tile]))
+    return pairs
 
 
 def outer_observations(state, at, rows_of):
@@ -328,14 +364,14 @@
     ws_ref[at : at + DROWS] = jnp.zeros((DROWS, *ws_ref.shape[1:]), jnp.float32)
     for row in range(DROWS):
         for tile in range(2):
-            vs_ref[at + row, tile] = -rows_of(row, tile)
+            vs_ref[at + row, tile] = rows_of(row, tile)
 
 
 def strip_kernel(
     xl_ref, tn_ref, lo_ref, hi_ref, dlo_ref, dhi_ref, wa_ref, va_ref, wb_ref, vb_ref, coef_ref,
     x1_ref, l1_ref, x2_ref, l2_ref, up_ref, dn_ref, halo_ref, *state,
 ):
-    state, flat_ref = state[:7], state[7]
+    state, flat_ref, clo_ref, chi_ref, sem_ref = state[:7], *state[6:]
     xs_ref, ls_ref, ws_ref, vs_ref, p_ref = state[:5]
     rows, _, columns = wa_ref.shape
     obs = (wa_ref, va_ref, wb_ref, vb_ref)
@@ -343,35 +379,44 @@
     sub = sublane((SUB, columns))
     inner = STRIP - MARGIN
     total = 2 * STRIP
+    coef_copies = started(
+        [(lo_ref.at[EDGE:], clo_ref), (hi_ref.at[EDGE:], chi_ref)], sem_ref.at[0:2]
+    )
+    pairs = own_copies(state, MARGIN, xl_ref, tn_ref, obs, 0, MARGIN)
+    pairs += own_copies(state, STRIP + MARGIN, xl_ref, tn_ref, obs, rows - MARGIN, MARGIN)
+    for refs, xat, lat_at, dat in (
+        ((lo_ref, dlo_ref), 0, MARGIN - LROWS, MARGIN - DROWS),
+        ((hi_ref, dhi_ref), STRIP + inner, STRIP + inner, STRIP + inner),
+    ):
+        ws_ref[dat : dat + DROWS] = jnp.zeros((DROWS, *ws_ref.shape[1:]), jnp.float32)
+        for tile, ref in enumerate(refs):
+            for dest, at, start, count in (
+                (xs_ref, xat, 0, MARGIN),
+                (ls_ref, lat_at, MARGIN, LROWS),
+                (vs_ref, dat, MARGIN + LROWS, DROWS),
+            ):
+                pairs.append((ref.at[start : start + count], dest.at[at : at + count, tile]))
+    copies = started(pairs, sem_ref.at[2:])
+    for copy in coef_copies:
+        copy.wait()
     for kind in range(3):
         for row in range(MARGIN):
             at = kind * MARGIN + row
-            for base, ref in ((0, lo_ref), (MARGIN, hi_ref)):
+            for base, ref in ((0, clo_ref), (MARGIN, chi_ref)):
                 halo_ref[kind, base + row : base + row + 1, :] = ref[
-                    EDGE + at // SUB, at % SUB : at % SUB + 1, :
+                    at // SUB, at % SUB : at % SUB + 1, :
                 ]
         flat_ref[kind, 0:MARGIN, :] = halo_ref[kind, 0:MARGIN, :]
         flat_ref[kind, MARGIN:STRIP, :] = coef_ref[kind, 0:inner, :]
         flat_ref[kind, STRIP : STRIP + inner, :] = coef_ref[kind, rows - inner : rows, :]
         flat_ref[kind, STRIP + inner : total, :] = halo_ref[kind, MARGIN : 2 * MARGIN, :]
-    widen_coefficients(
+    fold_coefficients(
         flat_ref,
-        state[6],
         total,
         (lambda at: jnp.where(at < STRIP, at - MARGIN, at - STRIP + rows - inner), rows),
     )
-    load_own(state, MARGIN, xl_ref, tn_ref, obs, 0, MARGIN)
-    load_own(state, STRIP + MARGIN, xl_ref, tn_ref, obs, rows - MARGIN, MARGIN)
-    for refs, xat, lat_at, dat in (
-        ((lo_ref, dlo_ref), 0, MARGIN - LROWS, MARGIN - DROWS),
-        ((hi_ref, dhi_ref), STRIP + inner, STRIP + inner, STRIP + inner),
-    ):
-        for tile, ref in enumerate(refs):
-            xs_ref[xat : xat + MARGIN, tile] = ref[0:MARGIN]
-            ls_ref[lat_at : lat_at + LROWS, tile] = ref[MARGIN : MARGIN + LROWS]
-        outer_observations(
-            state, dat, lambda row, tile, refs=refs: refs[tile][MARGIN + LROWS + row]
-        )
+    for copy in copies:
+        copy.wait()
     keep = jnp.logical_not(last)
     sweep(state, 0, STRIP + MARGIN, 2 * MARGIN, keep)
     for dest, ref in ((xs_ref, x1_ref), (ls_ref, l1_ref)):
@@ -399,7 +444,7 @@
         for row in range(DROWS):
             at = dat + row
             for tile in range(2):
-                p_ref[at, tile] = ws_ref[at, tile] * xs_ref[at, tile] - vs_ref[at, tile]
+                p_ref[at, tile] = vs_ref[at, tile] - ws_ref[at, tile] * xs_ref[at, tile]
         wide = narrow = 0
         for src, at, count, pair_at in (
             (xs_ref, xat, MARGIN, xat),
@@ -418,14 +463,17 @@
 def middle_kernel(
     xl_ref, tn_ref, wa_ref, va_ref, wb_ref, vb_ref, coef_ref, x1_ref, l1_ref, *state
 ):
-    state, flat_ref = state[:7], state[7]
+    state, flat_ref, sem_ref = state[:7], state[6], state[7]
     xs_ref, ls_ref = state[:2]
     rows = wa_ref.shape[0]
+    obs = (wa_ref, va_ref, wb_ref, vb_ref)
+    copies = started(own_copies(state, 0, xl_ref, tn_ref, obs, 0, rows), sem_ref)
     _, last = time_ends()
     for kind in range(3):
         flat_ref[kind, 0:rows, :] = coef_ref[kind]
-    widen_coefficients(flat_ref, state[6], rows, (lambda at: at, rows))
-    load_own(state, 0, xl_ref, tn_ref, (wa_ref, va_ref, wb_ref, vb_ref), 0, rows)
+    fold_coefficients(flat_ref, rows, (lambda at: at, rows))
+    for copy in copies:
+        copy.wait()
     sweep(state, 0, 0, rows, jnp.logical_not(last))
     x1_ref[...] = xs_ref[DROWS : rows - DROWS]
     l1_ref[...] = ls_ref[DROWS : rows - DROWS]
@@ -435,14 +483,14 @@
     xstrip_ref, lstrip_ref, x1_ref, l1_ref, wa_ref, va_ref, wb_ref, vb_ref, coef_ref,
     x3_ref, l3_ref, *state,
 ):
-    state, flat_ref = state[:7], state[7]
+    state, flat_ref = state[:7], state[6]
     xs_ref, ls_ref, ws_ref, vs_ref = state[:4]
     rows, _, columns = wa_ref.shape
     first, last = time_ends()
     sub = sublane((SUB, columns))
     for kind in range(3):
         flat_ref[kind, 0:rows, :] = coef_ref[kind]
-    widen_coefficients(flat_ref, state[6], rows, (lambda at: at, rows))
+    fold_coefficients(flat_ref, rows, (lambda at: at, rows))
     for tile, w, v in ((0, wa_ref, va_ref), (1, wb_ref, vb_ref)):
         ws_ref[0:rows, tile] = w[...]
         vs_ref[0:rows, tile] = v[...]
@@ -468,7 +516,7 @@
     xstrip_ref, lstrip_ref, x3_ref, l3_ref, lo_ref, hi_ref, wa_ref, va_ref, wb_ref, vb_ref,
     coef_ref, halo_ref, xout_ref, lout_ref, *state,
 ):
-    state, flat_ref, lines_ref = state[:7], state[7], state[8]
+    state, flat_ref, lines_ref = state[:7], state[6], state[7]
     xs_ref, ls_ref, ws_ref, vs_ref = state[:4]
     rows, _, columns = wa_ref.shape
     first, last = time_ends()
@@ -478,7 +526,7 @@
         flat_ref[kind, 0:MARGIN, :] = halo_ref[kind, 0:MARGIN, :]
         flat_ref[kind, MARGIN:top, :] = coef_ref[kind]
         flat_ref[kind, top : top + MARGIN, :] = halo_ref[kind, MARGIN : 2 * MARGIN, :]
-    widen_coefficients(flat_ref, state[6], rows + 2 * MARGIN, (lambda at: at - MARGIN, rows))
+    fold_coefficients(flat_ref, rows + 2 * MARGIN, (lambda at: at - MARGIN, rows))
     for dest, strip in ((xs_ref, xstrip_ref), (ls_ref, lstrip_ref)):
         dest[MARGIN : 2 * MARGIN] = strip[0:MARGIN]
         dest[top - MARGIN : top] = strip[MARGIN : 2 * MARGIN]
@@ -516,28 +564,25 @@
     sweep(state, 0, rows, 2 * MARGIN, keep, first & (sub < 4))
     xs_ref[MARGIN + DROWS : top - DROWS] = x3_ref[...]
     ls_ref[MARGIN + DROWS : top - DROWS] = l3_ref[...]
-    sweep(state, DROWS, 0, rows + 2 * DROWS, keep)
-
     parts = columns // LANES
-    for ref, dest in ((xs_ref, xout_ref), (ls_ref, lout_ref)):
-
-        def gather(step, carry, ref=ref):
-            value = jnp.where(
-                sub < 4,
-                rolled(ref[MARGIN + step, 0], 4, 0),
-                rolled(ref[MARGIN + step, 1], 4, 0),
-            )
+
+    def emit(at, new, lagrange):
+        start = (at - MARGIN) * SUB
+        for index, value in enumerate((new, lagrange)):
             for part in range(parts):
-                lines_ref[part, pl.ds(pl.multiple_of(step * SUB, SUB), SUB), :] = value[
+                lines_ref[index, part, pl.ds(start, SUB), :] = value[
                     :, part * LANES : (part + 1) * LANES
                 ]
-            return carry
-
-        lax.fori_loop(0, rows, gather, 0, unroll=4)
+
+    sweep(state, DROWS, 0, rows + 2 * DROWS, keep, emit=emit)
+    for index, dest in enumerate((xout_ref, lout_ref)):
         value = jnp.concatenate(
             [
                 jnp.concatenate(
-                    [lines_ref[part, pl.ds(slot, rows, stride=SUB), :] for part in range(parts)],
+                    [
+                        lines_ref[index, part, pl.ds(slot, rows, stride=SUB), :]
+                        for part in range(parts)
+                    ],
                     axis=1,
                 )
                 for slot in range(SUB)
@@ -577,7 +622,7 @@
     def call(kernel, outs, args, scratch=(), hbm=()):
         specs = [vmem] * len(args)
         for index in hbm:
-            specs[index] = pl.BlockSpec(memory_space=pl.ANY)
+            specs[index] = pl.BlockSpec(memory_space=pltpu.HBM)
         return pl.pallas_call(
             kernel,
             out_shape=[jax.ShapeDtypeStruct(shape, jnp.float32) for shape in outs],
@@ -595,7 +640,6 @@
     def state(length):
         return (
             [pltpu.VMEM((length + 2, 2, *tile), jnp.float32)] * 6
-            + [pltpu.VMEM((9, length + 2, *tile), jnp.float32)]
             + [pltpu.VMEM((12, length, columns), jnp.float32)]
         )
 
@@ -613,7 +657,11 @@
         edge_kernel,
         ([(EDGE + coef_rows, *tile)] * 2 + [(EDGE, *tile)] * 2),
         (xl, coef, *obs),
-        [pltpu.VMEM((edge_rows, *tile), jnp.float32)] * 2 + [edge_lines] * 2,
+        [pltpu.VMEM((edge_rows, *tile), jnp.float32)] * 2
+        + [edge_lines] * 2
+        + [pltpu.VMEM((2 * MARGIN, *tile), jnp.float32)] * 2
+        + [pltpu.SemaphoreType.DMA((4,))],
+        hbm=(0,),
     )
     lo = send(up, 0, 1)
     hi = send(dn, 0, -1)
@@ -628,12 +676,21 @@
     )
     outer = (2 * MARGIN, 2, *tile)
     inner = (rows - 2 * DROWS, 2, *tile)
-    x1, l1 = call(middle_kernel, (inner, inner), (xl, tn, *obs, coef), state(rows))
+    x1, l1 = call(
+        middle_kernel,
+        (inner, inner),
+        (xl, tn, *obs, coef),
+        state(rows) + [pltpu.SemaphoreType.DMA((8,))],
+        hbm=range(6),
+    )
     xstrip, lstrip, up, dn, halo = call(
         strip_kernel,
         (outer, outer, *[(EDGE + PAIRS, *tile)] * 2, (3, 2 * MARGIN, columns)),
         (xl, tn, lo, hi, dlo, dhi, *obs, coef, x1, l1),
-        state(2 * STRIP),
+        state(2 * STRIP)
+        + [pltpu.VMEM((coef_rows, *tile), jnp.float32)] * 2
+        + [pltpu.SemaphoreType.DMA((30,))],
+        hbm=range(10),
     )
     lo = send(up, 0, 1)
     hi = send(dn, 0, -1)
@@ -645,7 +702,8 @@
             final_kernel,
             (states.shape, states.shape),
             (xstrip, lstrip, x3, l3, lo, hi, *obs, coef, halo),
-            state(rows + 2 * MARGIN) + [lines],
+            state(rows + 2 * MARGIN)
+            + [pltpu.VMEM((2, columns // LANES, rows * SUB, LANES), jnp.float32)],
         )
     )
 

time: 76.6 us -> 72 us (0.940)
  Pallas kernels: 47 us -> 41.1 us
  waiting for transfers between devices: 4.24 us -> 5.41 us
    pallas_call x7, Pallas kernels: 47 us -> 41.1 us  [call(): pl.pallas_call(kernel, out_shape=[jax.ShapeDtypeStruct(shape, jnp.float32...]
    ppermute x7, waiting for transfers between devices: 4.24 us -> 5.41 us  [send(): return lax.ppermute(value, ('tm', 'lat'), pairs)]
  transfers between devices with their start and end apart: 7 -> 7, of which waited for: 1 -> 1; matrix products, arithmetic and copies ran while one was open for 0% -> 0% of each run, Pallas kernels for 35% -> 32%
where the time goes in v2:
time: 72 us; the launch traced here: 71.5 us
  Pallas kernels  41.1 us (57%)
  starting transfers between devices  21.6 us (30%)
  waiting for transfers between devices  5.41 us (8%)
  local copies, waits for them, and re-layouts  2.63 us (4%)
  between operations  0.8 us (1%)
    pallas_call x7, Pallas kernels, call(): pl.pallas_call(kernel, out_shape=[jax.ShapeDtypeStruct(shape, jnp.float32...  41.1 us
    ppermute x7, starting transfers between devices, send(): return lax.ppermute(value, ('tm', 'lat'), pairs)  21.6 us
    ppermute x7, waiting for transfers between devices, send(): return lax.ppermute(value, ('tm', 'lat'), pairs)  5.41 us
    unnamed x14, local copies, waits for them, and re-layouts  2.63 us
  transfers between devices with their start and end apart: 7, of which 1 were waited for; matrix products, arithmetic and copies ran while one was open for 0% of the time, Pallas kernels for 32%

profile of v2, /device:TPU:27, one launch (start us, length us, event | category | flops | bytes accessed | tf_op | source)
XLA Modules:
  0.0 71.5 jit_solution(4326954609965786043)
XLA Ops:
  0.6 3.2 %shard_map.122 = (f32[140,8,256]{2,1,0:T(8,128)}, f32[3,64,256]{2,1,0:T(8,128)}) custom-call(f32[8,64,256]{2,1,0:T(8,128)} %x_ref.1, f32[8,64,256]{2,1,0:T(8,128)} %l_ref.1, f32[64,256]{1,0:T(8,128)} %d_ref.1, f32[64,256]{1,0:T(8,128)} %z_ref.1, f32[64,256]{1,0:T(8,128)} %m_ref.1, s32[8,1,1024]{2,1,0:T(1,128)} %cells_ref.5, f32[8,1,1024]{2,1,0:T(1,128)} %values_ref.5, ...), custom_call_target="tpu_custom_call" | custom-call | tf_op jit(solution)/shard_map/pallas_call | solution.py:626
  3.8 2.6 %collective-permute-start = (f32[140,8,256]{2,1,0:T(8,128)}, f32[140,8,256]{2,1,0:T(8,128)S(1)}, u32[]{:S(2)}, u32[]{:S(2)}) collective-permute-start(f32[140,8,256]{2,1,0:T(8,128)} %get-tuple-element.21.xl_ref), channel_id=1, source_target_pairs={{8,0},{9,1},{10,2},{11,3},{12,4},{13,5},{14,6},{15,7},{16,8},{17,9... | collective-permute-start | bytes 3440648 | tf_op jit(solution)/shard_map/ppermute | solution.py:618
  6.5 3.3 %shard_map.123 = (f32[32,8,256]{2,1,0:T(8,128)}, f32[32,8,256]{2,1,0:T(8,128)}, f32[27,8,256]{2,1,0:T(8,128)}, f32[27,8,256]{2,1,0:T(8,128)}) custom-call(f32[140,8,256]{2,1,0:T(8,128)} %get-tuple-element.21.xl_ref, f32[3,64,256]{2,1,0:T(8,128)} %get-tuple-element.22.coef_ref, s32[8,1,1024]{2,1,0:T(1,128)} %cells_ref.5, f32[8,1,1024]{2,1,0:T(1,128)} %values_ref.5, ...), custom_call_target="tpu_custom_call" | custom-call | tf_op jit(solution)/shard_map/pallas_call | solution.py:626
  9.8 3.1 %collective-permute-start.1 = (f32[32,8,256]{2,1,0:T(8,128)}, f32[32,8,256]{2,1,0:T(8,128)S(1)}, u32[]{:S(2)}, u32[]{:S(2)}) collective-permute-start(f32[32,8,256]{2,1,0:T(8,128)} %get-tuple-element.23), channel_id=1, source_target_pairs={{0,1},{1,2},{2,3},{3,4},{4,5},{5,6},{6,7},{8,9},{9,10},{10,11},{11... | collective-permute-start | bytes 786440 | tf_op jit(solution)/shard_map/ppermute | solution.py:618
  13.0 3.0 %collective-permute-start.2 = (f32[32,8,256]{2,1,0:T(8,128)}, f32[32,8,256]{2,1,0:T(8,128)S(1)}, u32[]{:S(2)}, u32[]{:S(2)}) collective-permute-start(f32[32,8,256]{2,1,0:T(8,128)} %get-tuple-element.24), channel_id=1, source_target_pairs={{1,0},{2,1},{3,2},{4,3},{5,4},{6,5},{7,6},{9,8},{10,9},{11,10},{12... | collective-permute-start | bytes 786440 | tf_op jit(solution)/shard_map/ppermute | solution.py:618
  16.0 2.7 %collective-permute-start.3 = (f32[27,8,256]{2,1,0:T(8,128)}, f32[27,8,256]{2,1,0:T(8,128)S(1)}, u32[]{:S(2)}, u32[]{:S(2)}) collective-permute-start(f32[27,8,256]{2,1,0:T(8,128)} %get-tuple-element.25), channel_id=1, source_target_pairs={{8,1},{9,2},{10,3},{11,4},{12,5},{13,6},{14,7},{16,9},{17,10},{18,... | collective-permute-start | bytes 663560 | tf_op jit(solution)/shard_map/ppermute | solution.py:618
  18.7 3.7 %collective-permute-start.4 = (f32[27,8,256]{2,1,0:T(8,128)}, f32[27,8,256]{2,1,0:T(8,128)S(1)}, u32[]{:S(2)}, u32[]{:S(2)}) collective-permute-start(f32[27,8,256]{2,1,0:T(8,128)} %get-tuple-element.26), channel_id=1, source_target_pairs={{9,0},{10,1},{11,2},{12,3},{13,4},{14,5},{15,6},{17,8},{18,9},{19,... | collective-permute-start | bytes 663560 | tf_op jit(solution)/shard_map/ppermute | solution.py:618
  22.4 0.0 collective-permute-done.tn_ref
  22.4 0.0 copy-start
  22.4 1.0 %copy-done = f32[140,8,256]{2,1,0:T(8,128)} copy-done((f32[140,8,256]{2,1,0:T(8,128)}, f32[140,8,256]{2,1,0:T(8,128)S(1)}, u32[]{:S(2)}) %copy-start) | copy-done | bytes 1146904
  23.4 5.1 %shard_map.124 = (f32[64,8,256]{2,1,0:T(8,128)}, f32[64,8,256]{2,1,0:T(8,128)}, f32[64,8,256]{2,1,0:T(8,128)}, f32[64,8,256]{2,1,0:T(8,128)}) custom-call(f32[140,8,256]{2,1,0:T(8,128)} %copy-done, s32[8,1,1024]{2,1,0:T(1,128)} %cells_ref.5, f32[8,1,1024]{2,1,0:T(1,128)} %values_ref.5, f32[8,1,1024]{2,1,0:T(1,128)} %weights_ref.5, s32[4,1,1024]{2,1,0:T(1,128)} %refs_0_.1, ...), custom_call_target="tpu_custom_call" | custom-call | tf_op jit(solution)/shard_map/pallas_call | solution.py:626
  28.5 6.5 %shard_map.125 = (f32[52,2,8,256]{3,2,1,0:T(8,128)}, f32[52,2,8,256]{3,2,1,0:T(8,128)}) custom-call(f32[140,8,256]{2,1,0:T(8,128)} %get-tuple-element.21.xl_ref, f32[140,8,256]{2,1,0:T(8,128)} %copy-done, f32[64,8,256]{2,1,0:T(8,128)} %get-tuple-element.27.wa_ref, f32[64,8,256]{2,1,0:T(8,128)} %get-tuple-element.28.va_ref, ...), custom_call_target="tpu_custom_call" | custom-call | tf_op jit(solution)/shard_map/pallas_call | solution.py:626
  34.9 0.0 collective-permute-done.3.dlo_ref
  35.0 0.0 copy-start.5
  35.0 0.0 collective-permute-done.4.dhi_ref
  35.0 0.0 copy-start.6
  35.0 0.0 collective-permute-done.1.lo_ref
  35.0 0.0 copy-start.3
  35.0 0.0 collective-permute-done.2.hi_ref
  35.0 0.0 copy-start.4
  35.0 0.6 copy-done.5
  35.6 0.1 copy-done.6
  35.7 0.1 copy-done.3
  35.8 0.1 copy-done.4
  35.9 7.2 %shard_map.126 = (f32[24,2,8,256]{3,2,1,0:T(8,128)}, f32[24,2,8,256]{3,2,1,0:T(8,128)}, f32[41,8,256]{2,1,0:T(8,128)}, f32[41,8,256]{2,1,0:T(8,128)}, f32[3,24,256]{2,1,0:T(8,128)}) custom-call(f32[140,8,256]{2,1,0:T(8,128)} %get-tuple-element.21.xl_ref, f32[140,8,256]{2,1,0:T(8,128)} %copy-done, f32[32,8,256]{2,1,0:T(8,128)} %copy-done.3, ...), custom_call_target="tpu_custom_call" | custom-call | tf_op jit(solution)/shard_map/pallas_call | solution.py:626
  43.2 1.9 %collective-permute-start.5 = (f32[41,8,256]{2,1,0:T(8,128)}, f32[41,8,256]{2,1,0:T(8,128)S(1)}, u32[]{:S(2)}, u32[]{:S(2)}) collective-permute-start(f32[41,8,256]{2,1,0:T(8,128)} %get-tuple-element.37), channel_id=1, source_target_pairs={{0,1},{1,2},{2,3},{3,4},{4,5},{5,6},{6,7},{8,9},{9,10},{10,11},{11... | collective-permute-start | bytes 1007624 | tf_op jit(solution)/shard_map/ppermute | solution.py:618
  45.1 4.4 %collective-permute-start.6 = (f32[41,8,256]{2,1,0:T(8,128)}, f32[41,8,256]{2,1,0:T(8,128)S(1)}, u32[]{:S(2)}, u32[]{:S(2)}) collective-permute-start(f32[41,8,256]{2,1,0:T(8,128)} %get-tuple-element.38), channel_id=1, source_target_pairs={{1,0},{2,1},{3,2},{4,3},{5,4},{6,5},{7,6},{9,8},{10,9},{11,10},{12... | collective-permute-start | bytes 1007624 | tf_op jit(solution)/shard_map/ppermute | solution.py:618
  49.5 8.3 %shard_map.127 = (f32[52,2,8,256]{3,2,1,0:T(8,128)}, f32[52,2,8,256]{3,2,1,0:T(8,128)}) custom-call(f32[24,2,8,256]{3,2,1,0:T(8,128)} %get-tuple-element.33.xstrip_ref, f32[24,2,8,256]{3,2,1,0:T(8,128)} %get-tuple-element.34.lstrip_ref, f32[52,2,8,256]{3,2,1,0:T(8,128)} %get-tuple-element.31.x1_ref, f32[52,2,8,256]{3,2,1,0:T(8,128)} %get-tuple-element.32.l1_ref, ...), custom_call_target="tpu_custom_call" | custom-call | tf_op jit(solution)/shard_map/pallas_call | solution.py:626
  57.8 0.0 collective-permute-done.5.lo_ref
  57.8 5.4 %collective-permute-done.6.hi_ref = f32[41,8,256]{2,1,0:T(8,128)S(1)} collective-permute-done((f32[41,8,256]{2,1,0:T(8,128)}, f32[41,8,256]{2,1,0:T(8,128)S(1)}, u32[]{:S(2)}, u32[]{:S(2)}) %collective-permute-start.6) | collective-permute-done | bytes 335904 | tf_op jit(solution)/shard_map/ppermute | solution.py:618
  63.2 0.7 %copy-done.2 = f32[41,8,256]{2,1,0:T(8,128)} copy-done((f32[41,8,256]{2,1,0:T(8,128)}, f32[41,8,256]{2,1,0:T(8,128)S(1)}, u32[]{:S(2)}) %copy-start.2) | copy-done | bytes 335896
  64.0 7.5 %shard_map.128 = (f32[8,64,256]{2,1,0:T(8,128)}, f32[8,64,256]{2,1,0:T(8,128)}) custom-call(f32[24,2,8,256]{3,2,1,0:T(8,128)} %get-tuple-element.33.xstrip_ref, f32[24,2,8,256]{3,2,1,0:T(8,128)} %get-tuple-element.34.lstrip_ref, f32[52,2,8,256]{3,2,1,0:T(8,128)} %get-tuple-element.35.x3_ref, f32[52,2,8,256]{3,2,1,0:T(8,128)} %get-tuple-element.36.l3_ref, ...), custom_call_target="tpu_custom_call" | custom-call | tf_op jit(solution)/shard_map/pallas_call | solution.py:626
  (3 shorter events, 0.0 us)
Async XLA Ops:
  3.8 18.6 %collective-permute-start = (f32[140,8,256]{2,1,0:T(8,128)}, f32[140,8,256]{2,1,0:T(8,128)S(1)}, u32[]{:S(2)}, u32[]{:S(2)}) collective-permute-start(f32[140,8,256]{2,1,0:T(8,128)} %get-tuple-element.21.xl_ref), channel_id=1, source_target_pairs={{8,0},{9,1},{10,2},{11,3},{12,4},{13,5},{14,6},{15,7},{16,8},{17,9... | collective-permute-start | bytes 3440648 | tf_op jit(solution)/shard_map/ppermute | solution.py:618
  9.8 25.2 %collective-permute-start.1 = (f32[32,8,256]{2,1,0:T(8,128)}, f32[32,8,256]{2,1,0:T(8,128)S(1)}, u32[]{:S(2)}, u32[]{:S(2)}) collective-permute-start(f32[32,8,256]{2,1,0:T(8,128)} %get-tuple-element.23), channel_id=1, source_target_pairs={{0,1},{1,2},{2,3},{3,4},{4,5},{5,6},{6,7},{8,9},{9,10},{10,11},{11... | collective-permute-start | bytes 786440 | tf_op jit(solution)/shard_map/ppermute | solution.py:618
  13.0 22.1 %collective-permute-start.2 = (f32[32,8,256]{2,1,0:T(8,128)}, f32[32,8,256]{2,1,0:T(8,128)S(1)}, u32[]{:S(2)}, u32[]{:S(2)}) collective-permute-start(f32[32,8,256]{2,1,0:T(8,128)} %get-tuple-element.24), channel_id=1, source_target_pairs={{1,0},{2,1},{3,2},{4,3},{5,4},{6,5},{7,6},{9,8},{10,9},{11,10},{12... | collective-permute-start | bytes 786440 | tf_op jit(solution)/shard_map/ppermute | solution.py:618
  16.0 18.9 %collective-permute-start.3 = (f32[27,8,256]{2,1,0:T(8,128)}, f32[27,8,256]{2,1,0:T(8,128)S(1)}, u32[]{:S(2)}, u32[]{:S(2)}) collective-permute-start(f32[27,8,256]{2,1,0:T(8,128)} %get-tuple-element.25), channel_id=1, source_target_pairs={{8,1},{9,2},{10,3},{11,4},{12,5},{13,6},{14,7},{16,9},{17,10},{18,... | collective-permute-start | bytes 663560 | tf_op jit(solution)/shard_map/ppermute | solution.py:618
  18.7 16.3 %collective-permute-start.4 = (f32[27,8,256]{2,1,0:T(8,128)}, f32[27,8,256]{2,1,0:T(8,128)S(1)}, u32[]{:S(2)}, u32[]{:S(2)}) collective-permute-start(f32[27,8,256]{2,1,0:T(8,128)} %get-tuple-element.26), channel_id=1, source_target_pairs={{9,0},{10,1},{11,2},{12,3},{13,4},{14,5},{15,6},{17,8},{18,9},{19,... | collective-permute-start | bytes 663560 | tf_op jit(solution)/shard_map/ppermute | solution.py:618
  22.4 1.0 %copy-start = (f32[140,8,256]{2,1,0:T(8,128)}, f32[140,8,256]{2,1,0:T(8,128)S(1)}, u32[]{:S(2)}) copy-start(f32[140,8,256]{2,1,0:T(8,128)S(1)} %collective-permute-done.tn_ref) | copy-start | bytes 3440644
  35.0 0.7 copy-start.5
  35.0 0.7 %copy-start.6 = (f32[27,8,256]{2,1,0:T(8,128)}, f32[27,8,256]{2,1,0:T(8,128)S(1)}, u32[]{:S(2)}) copy-start(f32[27,8,256]{2,1,0:T(8,128)S(1)} %collective-permute-done.4.dhi_ref) | copy-start | bytes 663556
  35.0 0.8 %copy-start.3 = (f32[32,8,256]{2,1,0:T(8,128)}, f32[32,8,256]{2,1,0:T(8,128)S(1)}, u32[]{:S(2)}) copy-start(f32[32,8,256]{2,1,0:T(8,128)S(1)} %collective-permute-done.1.lo_ref) | copy-start | bytes 786436
  35.0 0.9 %copy-start.4 = (f32[32,8,256]{2,1,0:T(8,128)}, f32[32,8,256]{2,1,0:T(8,128)S(1)}, u32[]{:S(2)}) copy-start(f32[32,8,256]{2,1,0:T(8,128)S(1)} %collective-permute-done.2.hi_ref) | copy-start | bytes 786436
  43.2 14.7 %collective-permute-start.5 = (f32[41,8,256]{2,1,0:T(8,128)}, f32[41,8,256]{2,1,0:T(8,128)S(1)}, u32[]{:S(2)}, u32[]{:S(2)}) collective-permute-start(f32[41,8,256]{2,1,0:T(8,128)} %get-tuple-element.37), channel_id=1, source_target_pairs={{0,1},{1,2},{2,3},{3,4},{4,5},{5,6},{6,7},{8,9},{9,10},{10,11},{11... | collective-permute-start | bytes 1007624 | tf_op jit(solution)/shard_map/ppermute | solution.py:618
  45.1 18.1 %collective-permute-start.6 = (f32[41,8,256]{2,1,0:T(8,128)}, f32[41,8,256]{2,1,0:T(8,128)S(1)}, u32[]{:S(2)}, u32[]{:S(2)}) collective-permute-start(f32[41,8,256]{2,1,0:T(8,128)} %get-tuple-element.38), channel_id=1, source_target_pairs={{1,0},{2,1},{3,2},{4,3},{5,4},{6,5},{7,6},{9,8},{10,9},{11,10},{12... | collective-permute-start | bytes 1007624 | tf_op jit(solution)/shard_map/ppermute | solution.py:618
  57.8 5.4 %copy-start.1 = (f32[41,8,256]{2,1,0:T(8,128)}, f32[41,8,256]{2,1,0:T(8,128)S(1)}, u32[]{:S(2)}) copy-start(f32[41,8,256]{2,1,0:T(8,128)S(1)} %collective-permute-done.5.lo_ref) | copy-start | bytes 1007620
  63.2 0.7 %copy-start.2 = (f32[41,8,256]{2,1,0:T(8,128)}, f32[41,8,256]{2,1,0:T(8,128)S(1)}, u32[]{:S(2)}) copy-start(f32[41,8,256]{2,1,0:T(8,128)S(1)} %collective-permute-done.6.hi_ref) | copy-start | bytes 1007620
